TPU v7x, 32 devices: a whole 2x2x4 slice. The times are simulated.
32 devices in a mesh: dp: 8 (over z, core), tensor: 4 (over y, x).
Axes of the slice: x: 2, y: 2, z: 4, core: 2. Of those that a mesh axis runs over, the one named last changes fastest.
Arguments:
- inputs: float32 [13848, 1024], P('dp'), may hold values from -6 to 6
- grad_out: float32 [13848, 1024], P('dp'), may hold values from -6 to 6
- w_qkv: bfloat16 [2, 3, 1024, 1024], P(None, None, 'dp', 'tensor'), may hold values from -0.1875 to 0.1875
- b_qv: bfloat16 [2, 2, 16, 64], P(None, None, 'tensor', 'dp'), may hold values from -3 to 3
- w_out: bfloat16 [2, 1024, 1024], P(None, 'tensor', 'dp'), may hold values from -0.75 to 0.75
- w_up: bfloat16 [2, 1024, 4096], P(None, 'dp', 'tensor'), may hold values from -0.1875 to 0.1875
- b_up: bfloat16 [2, 64, 64], P(None, 'tensor', 'dp'), may hold values from -3 to 3
- w_down: bfloat16 [2, 4096, 1024], P(None, 'tensor', 'dp'), may hold values from -0.09375 to 0.09375
- ln_gain: float32 [2, 2, 1024], P(None, None, ('dp', 'tensor')), may hold values from 0.1 to 1.9
- tok_bias: float32 [2, 4, 1024], P(None, None, ('dp', 'tensor')), may hold values from -3 to 3
Outputs:
- block_out: float32 [13848, 1024], P('dp')
- grad_in: float32 [13848, 1024], P('dp')
- grad_w_qkv: float32 [2, 3, 1024, 1024], P(None, None, 'dp', 'tensor')
- grad_b_qv: float32 [2, 2, 16, 64], P(None, None, 'tensor', 'dp')
- grad_w_out: float32 [2, 1024, 1024], P(None, 'tensor', 'dp')
- grad_w_up: float32 [2, 1024, 4096], P(None, 'dp', 'tensor')
- grad_b_up: float32 [2, 64, 64], P(None, 'tensor', 'dp')
- grad_w_down: float32 [2, 4096, 1024], P(None, 'tensor', 'dp')
- grad_ln_gain: float32 [2, 2, 1024], P(None, None, ('dp', 'tensor'))
- grad_tok_bias: float32 [2, 4, 1024], P(None, None, ('dp', 'tensor'))
All inputs are finite; a program needn't handle non-finite values.
Results may differ from a plain program's by a relative error of at most 0.02.
Values may be sent and summed in bfloat16 or wider, within the bound.
No kernel may reach another device: no remote copies, remote signals or barrier semaphores. Data moves between devices by JAX's collectives and lax.ppermute only.
A program may use at most 256 MiB of HBM per device.

v0:
```python
import jax
import jax.numpy as jnp
from jax import lax
from jax.sharding import PartitionSpec as P

HEAD_DIM = 64
SEQ = 577
LAYERS = 2


epsilon = 1e-05
root_half = 0.7071067811865476
inv_root_two_pi = 0.3989422804014327


def norm_forward(stream_rows, gain_row, shift_row):
    center = stream_rows - jnp.mean(stream_rows, axis=-1, keepdims=True)
    inverse = lax.rsqrt(jnp.mean(center * center, axis=-1, keepdims=True) + epsilon)
    normed = center * inverse
    return (normed * gain_row + shift_row, normed, inverse)


def norm_backward(upstream, gain_row, normed, inverse):
    scaled = upstream * gain_row
    mean_one = jnp.mean(scaled, axis=-1, keepdims=True)
    mean_two = jnp.mean(scaled * normed, axis=-1, keepdims=True)
    return (
        inverse * (scaled - mean_one - normed * mean_two),
        jnp.sum(upstream * normed, axis=0),
        jnp.sum(upstream, axis=0),
    )


def gelu_value(hidden):
    return hidden * (0.5 * (1.0 + lax.erf(hidden * root_half)))


def gelu_slope(hidden):
    return (
        0.5 * (1.0 + lax.erf(hidden * root_half))
        + hidden * jnp.exp(-0.5 * hidden * hidden) * inv_root_two_pi
    )


def attend_image(inputs):
    query_rows, key_rows, value_rows = inputs
    scores = jnp.einsum("qhd,khd->hqk", query_rows, key_rows, preferred_element_type=jnp.float32)
    row_peak = jnp.max(scores, axis=-1, keepdims=True)
    exponent = jnp.exp(scores - row_peak)
    totals = jnp.sum(exponent, axis=-1, keepdims=True)
    attn_probs = (exponent / totals).astype(jnp.bfloat16)
    mixed_heads = jnp.einsum(
        "hqk,khd->qhd", attn_probs, value_rows, preferred_element_type=jnp.float32
    )
    return (mixed_heads.astype(jnp.bfloat16), (row_peak + jnp.log(totals))[..., 0])


def attend_back(inputs):
    query_rows, key_rows, value_rows, log_total, grad_mixed = inputs
    scores = jnp.einsum("qhd,khd->hqk", query_rows, key_rows, preferred_element_type=jnp.float32)
    attn_probs = jnp.exp(scores - log_total[..., None])
    grad_probs = jnp.einsum(
        "qhd,khd->hqk", grad_mixed, value_rows, preferred_element_type=jnp.float32
    )
    inner_sum = jnp.sum(attn_probs * grad_probs, axis=-1, keepdims=True)
    grad_scores = (attn_probs * (grad_probs - inner_sum)).astype(jnp.bfloat16)
    grad_query = jnp.einsum(
        "hqk,khd->qhd", grad_scores, key_rows, preferred_element_type=jnp.float32
    ) * HEAD_DIM ** (-0.5)
    grad_key = jnp.einsum(
        "hqk,qhd->khd", grad_scores, query_rows, preferred_element_type=jnp.float32
    )
    grad_value = jnp.einsum(
        "hqk,qhd->khd",
        attn_probs.astype(jnp.bfloat16),
        grad_mixed,
        preferred_element_type=jnp.float32,
    )
    return jnp.stack([grad_query, grad_key, grad_value], axis=1)


def fetch_forward(qkv_part, qv_part, out_part, up_part, upb_part, down_part):
    return (
        lax.all_gather(qkv_part, "dp", axis=1, tiled=True),
        lax.all_gather(qv_part, "dp", axis=2, tiled=True),
        lax.all_gather(out_part, "dp", axis=1, tiled=True),
        lax.all_gather(up_part, "dp", axis=0, tiled=True),
        lax.all_gather(upb_part, "dp", axis=1, tiled=True),
        lax.all_gather(down_part, "dp", axis=1, tiled=True),
    )


def fetch_again(qkv_part, qv_part, out_part, up_part, upb_part, down_part):
    return (
        lax.all_gather(qkv_part, "dp", axis=1, tiled=True),
        lax.all_gather(qv_part, "dp", axis=2, tiled=True),
        lax.all_gather(out_part, "dp", axis=1, tiled=True),
        lax.all_gather(up_part, "dp", axis=0, tiled=True),
        lax.all_gather(upb_part, "dp", axis=1, tiled=True),
        lax.all_gather(down_part, "dp", axis=1, tiled=True),
    )


def pad_rows(rows, extra_rows):
    return jnp.pad(rows, ((0, extra_rows), (0, 0)))


def spread_rows(token_rows, group_rows):
    return lax.all_gather(token_rows, "tensor", axis=0, tiled=True)[:group_rows]


def gather_cotangent(token_rows, group_rows):
    return lax.all_gather(token_rows, "tensor", axis=0, tiled=True)[:group_rows]


def reduce_branch(partial_rows, extra_rows):
    return lax.psum_scatter(
        pad_rows(partial_rows, extra_rows).astype(jnp.bfloat16),
        "tensor",
        scatter_dimension=0,
        tiled=True,
    ).astype(jnp.float32)


def branch_output(local_rows, local_w, extra_rows):
    return reduce_branch(
        jnp.dot(local_rows, local_w, preferred_element_type=jnp.float32), extra_rows
    )


def reduce_input(partial_rows, extra_rows):
    return lax.psum_scatter(
        pad_rows(partial_rows, extra_rows).astype(jnp.bfloat16),
        "tensor",
        scatter_dimension=0,
        tiled=True,
    ).astype(jnp.float32)


def reduce_weights(grad_qkvw, grad_qv, grad_outw, grad_up, grad_upb, grad_down):
    return (
        lax.psum_scatter(
            grad_qkvw.astype(jnp.bfloat16), "dp", scatter_dimension=1, tiled=True
        ).astype(jnp.float32),
        lax.psum_scatter(
            grad_qv.astype(jnp.bfloat16), "dp", scatter_dimension=2, tiled=True
        ).astype(jnp.float32),
        lax.psum_scatter(
            grad_outw.astype(jnp.bfloat16), "dp", scatter_dimension=1, tiled=True
        ).astype(jnp.float32),
        lax.psum_scatter(
            grad_up.astype(jnp.bfloat16), "dp", scatter_dimension=0, tiled=True
        ).astype(jnp.float32),
        lax.psum_scatter(
            grad_upb.astype(jnp.bfloat16), "dp", scatter_dimension=1, tiled=True
        ).astype(jnp.float32),
        lax.psum_scatter(
            grad_down.astype(jnp.bfloat16), "dp", scatter_dimension=1, tiled=True
        ).astype(jnp.float32),
    )


def shards(inputs, grad_out, w_qkv, b_qv, w_out, w_up, b_up, w_down, ln_gain, tok_bias):
    gains, shifts = (
        lax.all_gather(ln_gain, ("dp", "tensor"), axis=2, tiled=True),
        lax.all_gather(tok_bias, ("dp", "tensor"), axis=2, tiled=True),
    )
    score_scale = HEAD_DIM ** (-0.5)
    group_rows = inputs.shape[0]
    tensor_count = lax.axis_size("tensor")
    share_rows = (group_rows + tensor_count - 1) // tensor_count
    extra_rows = share_rows * tensor_count - group_rows
    row_offset = lax.axis_index("tensor") * share_rows
    images = group_rows // SEQ
    stream = lax.dynamic_slice_in_dim(pad_rows(inputs, extra_rows), row_offset, share_rows, 0)
    cotangent = lax.dynamic_slice_in_dim(pad_rows(grad_out, extra_rows), row_offset, share_rows, 0)
    saved_list = []
    for block_index in range(LAYERS):
        fetched = fetch_forward(
            w_qkv[block_index],
            b_qv[block_index],
            w_out[block_index],
            w_up[block_index],
            b_up[block_index],
            w_down[block_index],
        )
        qkv_w, qv_bias, out_w, up_w, up_bias, down_w = fetched
        local_width = qkv_w.shape[2]
        image_shape = (images, SEQ, local_width // HEAD_DIM, HEAD_DIM)
        normed_one, hat_one, inv_one = norm_forward(
            stream, gains[block_index, 0], shifts[block_index, 0]
        )
        rows_one = normed_one.astype(jnp.bfloat16)
        whole_one = spread_rows(rows_one, group_rows)
        projected = jnp.einsum("td,jde->tje", whole_one, qkv_w, preferred_element_type=jnp.float32)
        biases = qv_bias.reshape(2, local_width).astype(jnp.float32)
        query_rows = ((projected[:, 0] + biases[0]) * score_scale).astype(jnp.bfloat16)
        key_rows = projected[:, 1].astype(jnp.bfloat16)
        value_rows = (projected[:, 2] + biases[1]).astype(jnp.bfloat16)
        mixed_heads, log_total = lax.map(
            attend_image,
            (
                query_rows.reshape(image_shape),
                key_rows.reshape(image_shape),
                value_rows.reshape(image_shape),
            ),
        )
        mixed_heads = mixed_heads.reshape(-1, local_width)
        middle = stream + branch_output(mixed_heads, out_w, extra_rows) + shifts[block_index, 1]
        normed_two, hat_two, inv_two = norm_forward(
            middle, gains[block_index, 1], shifts[block_index, 2]
        )
        rows_two = normed_two.astype(jnp.bfloat16)
        whole_two = spread_rows(rows_two, group_rows)
        hidden = jnp.dot(whole_two, up_w, preferred_element_type=jnp.float32) + up_bias.reshape(
            -1
        ).astype(jnp.float32)
        activation = gelu_value(hidden).astype(jnp.bfloat16)
        stream = middle + branch_output(activation, down_w, extra_rows) + shifts[block_index, 3]
        saved_list.append(
            (
                fetched,
                rows_one,
                whole_one,
                hat_one,
                inv_one,
                query_rows,
                key_rows,
                value_rows,
                log_total,
                mixed_heads,
                rows_two,
                whole_two,
                hat_two,
                inv_two,
                hidden,
                activation,
            )
        )
    weight_list = [None] * LAYERS
    gain_list = [None] * LAYERS
    shift_list = [None] * LAYERS
    for block_index in reversed(range(LAYERS)):
        (
            fetched,
            rows_one,
            whole_one,
            hat_one,
            inv_one,
            query_rows,
            key_rows,
            value_rows,
            log_total,
            mixed_heads,
            rows_two,
            whole_two,
            hat_two,
            inv_two,
            hidden,
            activation,
        ) = saved_list[block_index]
        qkv_w, qv_bias, out_w, up_w, up_bias, down_w = fetch_again(
            w_qkv[block_index],
            b_qv[block_index],
            w_out[block_index],
            w_up[block_index],
            b_up[block_index],
            w_down[block_index],
        )
        local_width = qkv_w.shape[2]
        local_heads = local_width // HEAD_DIM
        image_shape = (images, SEQ, local_heads, HEAD_DIM)
        shift_down = jnp.sum(cotangent, axis=0)
        whole_cot = gather_cotangent(cotangent.astype(jnp.bfloat16), group_rows)
        grad_down = jnp.einsum(
            "tf,td->fd", activation, whole_cot, preferred_element_type=jnp.float32
        )
        grad_hidden = jnp.einsum(
            "td,fd->tf", whole_cot, down_w, preferred_element_type=jnp.float32
        ) * gelu_slope(hidden)
        grad_upb = jnp.sum(grad_hidden, axis=0)
        hidden_rows = grad_hidden.astype(jnp.bfloat16)
        grad_up = jnp.einsum(
            "td,tf->df", whole_two, hidden_rows, preferred_element_type=jnp.float32
        )
        back_two = reduce_input(
            jnp.einsum("tf,df->td", hidden_rows, up_w, preferred_element_type=jnp.float32),
            extra_rows,
        )
        dstream, gain_two, shift_two = norm_backward(
            back_two, gains[block_index, 1], hat_two, inv_two
        )
        cotangent = cotangent + dstream
        shift_out = jnp.sum(cotangent, axis=0)
        whole_cot = gather_cotangent(cotangent.astype(jnp.bfloat16), group_rows)
        grad_outw = jnp.einsum(
            "te,td->ed", mixed_heads, whole_cot, preferred_element_type=jnp.float32
        )
        grad_mixed = jnp.einsum(
            "td,ed->te", whole_cot, out_w, preferred_element_type=jnp.float32
        ).astype(jnp.bfloat16)
        qkv_grads = lax.map(
            attend_back,
            (
                query_rows.reshape(image_shape),
                key_rows.reshape(image_shape),
                value_rows.reshape(image_shape),
                log_total,
                grad_mixed.reshape(image_shape),
            ),
        )
        qkv_grads = qkv_grads.reshape(-1, 3, local_width)
        grad_qv = jnp.stack(
            [jnp.sum(qkv_grads[:, 0], axis=0), jnp.sum(qkv_grads[:, 2], axis=0)]
        ).reshape(2, local_heads, HEAD_DIM)
        qkv_rows = qkv_grads.astype(jnp.bfloat16)
        grad_qkvw = jnp.einsum(
            "td,tje->jde", whole_one, qkv_rows, preferred_element_type=jnp.float32
        )
        back_one = reduce_input(
            jnp.einsum("tje,jde->td", qkv_rows, qkv_w, preferred_element_type=jnp.float32),
            extra_rows,
        )
        dstream, gain_one, shift_one = norm_backward(
            back_one, gains[block_index, 0], hat_one, inv_one
        )
        cotangent = cotangent + dstream
        weight_list[block_index] = reduce_weights(
            grad_qkvw, grad_qv, grad_outw, grad_up, grad_upb.reshape(up_bias.shape), grad_down
        )
        gain_list[block_index] = jnp.stack([gain_one, gain_two])
        shift_list[block_index] = jnp.stack([shift_one, shift_out, shift_two, shift_down])
    gain_total, shift_total = (
        lax.psum_scatter(jnp.stack(gain_list), ("dp", "tensor"), scatter_dimension=2, tiled=True),
        lax.psum_scatter(jnp.stack(shift_list), ("dp", "tensor"), scatter_dimension=2, tiled=True),
    )
    full_out, full_back = (
        lax.all_gather(stream.astype(jnp.bfloat16), "tensor", axis=0, tiled=True).astype(
            stream.dtype
        ),
        lax.all_gather(cotangent.astype(jnp.bfloat16), "tensor", axis=0, tiled=True).astype(
            cotangent.dtype
        ),
    )
    stacked = [
        jnp.stack([weight_list[block_index][member] for block_index in range(LAYERS)])
        for member in range(6)
    ]
    return (
        full_out[:group_rows],
        full_back[:group_rows],
        stacked[0],
        stacked[1],
        stacked[2],
        stacked[3],
        stacked[4],
        stacked[5],
        gain_total,
        shift_total,
    )


def solution(mesh):
    in_specs = (
        P("dp", None),
        P("dp", None),
        P(None, None, "dp", "tensor"),
        P(None, None, "tensor", "dp"),
        P(None, "tensor", "dp"),
        P(None, "dp", "tensor"),
        P(None, "tensor", "dp"),
        P(None, "tensor", "dp"),
        P(None, None, ("dp", "tensor")),
        P(None, None, ("dp", "tensor")),
    )
    out_specs = (
        P("dp", None),
        P("dp", None),
        P(None, None, "dp", "tensor"),
        P(None, None, "tensor", "dp"),
        P(None, "tensor", "dp"),
        P(None, "dp", "tensor"),
        P(None, "tensor", "dp"),
        P(None, "tensor", "dp"),
        P(None, None, ("dp", "tensor")),
        P(None, None, ("dp", "tensor")),
    )
    return jax.shard_map(shards, mesh=mesh, in_specs=in_specs, out_specs=out_specs, check_vma=False)
```

profile of v0, /device:TPU:0, one launch (start us, length us, event | category | flops | bytes accessed | tf_op | source)
XLA Modules:
  0.0 2272.8 jit_solution(16372932527335187734)
XLA Ops:
  11.7 75.6 %all_gather.81 = f32[2,4,1024]{1,0,2:T(2,128)S(1)} all-gather(f32[2,4,32]{1,0,2:T(2,128)S(1)} %copy.242), channel_id=1, replica_groups=mesh['dp'=8,'tensor'=4] {'dp','tensor'}, dimensions={2}, use_global_device_ids=true | all-gather | bytes 33792 | tf_op jit(solution)/shard_map/all_gather | solution.py:166
  87.3 27.6 %slice_reduce_fusion.4 = (f32[1024]{0:T(1024)}, f32[1024]{0:T(1024)}, f32[1024]{0:T(1024)}, f32[1024]{0:T(1024)}, f32[1024]{0:T(1024)}, /*index=5*/f32[1024]{0:T(1024)}, f32[1024]{0:T(1024)}, f32[1024]{0:T(1024)S(1)}) fusion(f32[2,4,1024]{1,0,2:T(2,128)S(1)} %all_gather.81), kind=kLoop, calls=%fused_computation.270 | loop fusion | bytes 65536 | tf_op jit(solution)/shard_map/slice | solution.py:219
  114.9 69.4 %all_gather.80 = f32[2,2,1024]{1,0,2:T(2,128)S(1)} all-gather(f32[2,2,32]{1,0,2:T(2,128)S(1)} %copy.241), channel_id=1, replica_groups=mesh['dp'=8,'tensor'=4] {'dp','tensor'}, dimensions={2}, use_global_device_ids=true | all-gather | bytes 16896 | tf_op jit(solution)/shard_map/all_gather | solution.py:165
  184.3 26.5 %slice_reduce_fusion.6 = (f32[1024]{0:T(1024)}, f32[1024]{0:T(1024)}, f32[1024]{0:T(1024)}, f32[1024]{0:T(1024)S(1)}) fusion(f32[2,2,1024]{1,0,2:T(2,128)S(1)} %all_gather.80), kind=kLoop, calls=%fused_computation.272 | loop fusion | bytes 32768 | tf_op jit(solution)/shard_map/slice | solution.py:211
  337.1 50.3 %fusion = bf16[448,1024]{1,0:T(8,128)(2,1)S(1)} fusion(bf16[1732,1024]{1,0:T(8,128)(2,1)} %pad.40), kind=kCustom, calls=%all-reduce-scatter | all-reduce-scatter fusion | flops 1835009 | bytes 4465152
  415.0 34.3 %all-gather.53.cloned.1.call-done = bf16[4,433,1024]{2,1,0:T(8,128)(2,1)} async-done(((bf16[1,433,1024]{2,1,0:T(8,128)(2,1)}), bf16[4,433,1024]{2,1,0:T(8,128)(2,1)}) %all-gather.53.cloned.1.call-update) | async-done | bytes 3547152 | tf_op jit(solution)/shard_map/all_gather | solution.py:109
  454.0 26.4 %all-gather.41.cloned.1.call-done = bf16[1,1024,1024]{2,1,0:T(8,128)(2,1)} async-done(((bf16[1,128,1024]{2,1,0:T(8,128)(2,1)}), bf16[1,1024,1024]{2,1,0:T(8,128)(2,1)}) %all-gather.41.cloned.1.call-update) | async-done | bytes 2097168 | tf_op jit(solution)/shard_map/all_gather | solution.py:87
  521.2 50.2 %fusion.1 = bf16[448,1024]{1,0:T(8,128)(2,1)S(1)} fusion(bf16[1732,1024]{1,0:T(8,128)(2,1)} %pad.41), kind=kCustom, calls=%all-reduce-scatter.1 | all-reduce-scatter fusion | flops 1835009 | bytes 4465152
  711.3 50.5 %fusion.2 = bf16[448,1024]{1,0:T(8,128)(2,1)S(1)} fusion(bf16[1732,1024]{1,0:T(8,128)(2,1)} %pad.42), kind=kCustom, calls=%all-reduce-scatter.2 | all-reduce-scatter fusion | flops 1835009 | bytes 4465152
  794.7 30.6 %all-gather.57.cloned.1.call-done = bf16[4,433,1024]{2,1,0:T(8,128)(2,1)} async-done(((bf16[1,433,1024]{2,1,0:T(8,128)(2,1)}), bf16[4,433,1024]{2,1,0:T(8,128)(2,1)}) %all-gather.57.cloned.1.call-update) | async-done | bytes 3547152 | tf_op jit(solution)/shard_map/all_gather | solution.py:109
  830.0 26.5 %all-gather.47.cloned.1.call-done = bf16[1,1024,1024]{2,1,0:T(8,128)(2,1)} async-done(((bf16[1,128,1024]{2,1,0:T(8,128)(2,1)}), bf16[1,1024,1024]{2,1,0:T(8,128)(2,1)}) %all-gather.47.cloned.1.call-update) | async-done | bytes 2097168 | tf_op jit(solution)/shard_map/all_gather | solution.py:87
  904.8 50.8 %fusion.4 = bf16[448,1024]{1,0:T(8,128)(2,1)} fusion(bf16[1732,1024]{1,0:T(8,128)(2,1)} %pad.45), kind=kCustom, calls=%all-reduce-scatter.4 | all-reduce-scatter fusion | flops 1835009 | bytes 4465152
  977.0 49.6 %all-gather.63.cloned.1.call-done = bf16[4,433,1024]{2,1,0:T(8,128)(2,1)} async-done(((bf16[1,433,1024]{2,1,0:T(8,128)(2,1)}), bf16[4,433,1024]{2,1,0:T(8,128)(2,1)}) %all-gather.63.cloned.1.call-update) | async-done | bytes 3547152 | tf_op jit(solution)/shard_map/all_gather | solution.py:113
  1045.1 152.0 %while.46 = (s32[]{:T(128)}, f32[3,577,3,4,64]{1,0,4,3,2:T(4,128)}, bf16[3,577,4,64]{1,3,2,0:T(8,128)(2,1)}, bf16[3,577,4,64]{1,3,2,0:T(8,128)(2,1)S(1)}, f32[3,...) while((s32[]{:T(128)}, f32[3,577,3,4,64]{1,0,4,3,2:T(4,128)}, ...), condition=%wide.region_25.26_spmd, body=%wide.region_23.25_spmd.sunk | while | flops 865315328 | bytes 55046488 | solution.py:302
  1057.7 38.1 %dynamic_update_slice.35 = f32[3,577,3,4,64]{1,0,4,3,2:T(4,128)} dynamic-update-slice(f32[3,577,3,4,64]{1,0,4,3,2:T(4,128)} %get-tuple-element.747, f32[1,577,3,4,64]{1,0,4,3,2:T(1,128)S(1)} %copy.368, s32[]{:T(128)S(6)} %copy.396, s32[]{:T(128)} %constant.102.clone.1..sunk, s32[]{:T(128)} %constant.102.clone.1..sunk, s32[]{:T(128)} %constant.102.clone.1..sunk, s32[]{:T(128)} %constant.102.clone.1..sunk) | dynamic-update-slice | bytes 3545092 | tf_op jit(solution)/shard_map/while/body/jit(dynamic_update_index_in_dim)/dynamic_update_slice | solution.py:302
  1108.4 38.1 %dynamic_update_slice.35 = f32[3,577,3,4,64]{1,0,4,3,2:T(4,128)} dynamic-update-slice(f32[3,577,3,4,64]{1,0,4,3,2:T(4,128)} %get-tuple-element.747, f32[1,577,3,4,64]{1,0,4,3,2:T(1,128)S(1)} %copy.368, s32[]{:T(128)S(6)} %copy.396, s32[]{:T(128)} %constant.102.clone.1..sunk, s32[]{:T(128)} %constant.102.clone.1..sunk, s32[]{:T(128)} %constant.102.clone.1..sunk, s32[]{:T(128)} %constant.102.clone.1..sunk) | dynamic-update-slice | bytes 3545092 | tf_op jit(solution)/shard_map/while/body/jit(dynamic_update_index_in_dim)/dynamic_update_slice | solution.py:302
  1159.1 38.1 %dynamic_update_slice.35 = f32[3,577,3,4,64]{1,0,4,3,2:T(4,128)} dynamic-update-slice(f32[3,577,3,4,64]{1,0,4,3,2:T(4,128)} %get-tuple-element.747, f32[1,577,3,4,64]{1,0,4,3,2:T(1,128)S(1)} %copy.368, s32[]{:T(128)S(6)} %copy.396, s32[]{:T(128)} %constant.102.clone.1..sunk, s32[]{:T(128)} %constant.102.clone.1..sunk, s32[]{:T(128)} %constant.102.clone.1..sunk, s32[]{:T(128)} %constant.102.clone.1..sunk) | dynamic-update-slice | bytes 3545092 | tf_op jit(solution)/shard_map/while/body/jit(dynamic_update_index_in_dim)/dynamic_update_slice | solution.py:302
  1218.9 51.2 %fusion.5 = bf16[448,1024]{1,0:T(8,128)(2,1)S(1)} fusion(bf16[1732,1024]{1,0:T(8,128)(2,1)} %pad.46), kind=kCustom, calls=%all-reduce-scatter.5 | all-reduce-scatter fusion | flops 1835009 | bytes 4465152
  1284.8 49.6 %all-gather.65.cloned.1.call-done = bf16[4,433,1024]{2,1,0:T(8,128)(2,1)} async-done(((bf16[1,433,1024]{2,1,0:T(8,128)(2,1)}), bf16[4,433,1024]{2,1,0:T(8,128)(2,1)}) %all-gather.65.cloned.1.call-update) | async-done | bytes 3547152 | tf_op jit(solution)/shard_map/all_gather | solution.py:113
  1354.6 51.2 %fusion.6 = bf16[448,1024]{1,0:T(8,128)(2,1)S(1)} fusion(bf16[1732,1024]{1,0:T(8,128)(2,1)} %pad.47), kind=kCustom, calls=%all-reduce-scatter.6 | all-reduce-scatter fusion | flops 1835009 | bytes 4465152
  1503.4 154.2 %while.47 = (s32[]{:T(128)}, f32[3,577,3,4,64]{1,0,4,3,2:T(4,128)}, bf16[3,577,4,64]{1,3,2,0:T(8,128)(2,1)}, bf16[3,577,4,64]{1,3,2,0:T(8,128)(2,1)S(1)}, f32[3,...) while((s32[]{:T(128)}, f32[3,577,3,4,64]{1,0,4,3,2:T(4,128)}, ...), condition=%wide.region_34.35_spmd, body=%wide.region_32.34_spmd.sunk | while | flops 865315328 | bytes 55046488 | solution.py:302
  1516.7 38.1 %dynamic_update_slice.36 = f32[3,577,3,4,64]{1,0,4,3,2:T(4,128)} dynamic-update-slice(f32[3,577,3,4,64]{1,0,4,3,2:T(4,128)} %get-tuple-element.774, f32[1,577,3,4,64]{1,0,4,3,2:T(1,128)S(1)} %copy.369, s32[]{:T(128)S(6)} %copy.402, s32[]{:T(128)} %constant.102.clone.1..sunk.1, s32[]{:T(128)} %constant.102.clone.1..sunk.1, s32[]{:T(128)} %constant.102.clone.1..sunk.1, s32[]{:T(128)} %constant.102.clone.1..sunk.1) | dynamic-update-slice | bytes 3545092 | tf_op jit(solution)/shard_map/while/body/jit(dynamic_update_index_in_dim)/dynamic_update_slice | solution.py:302
  1568.0 38.2 %dynamic_update_slice.36 = f32[3,577,3,4,64]{1,0,4,3,2:T(4,128)} dynamic-update-slice(f32[3,577,3,4,64]{1,0,4,3,2:T(4,128)} %get-tuple-element.774, f32[1,577,3,4,64]{1,0,4,3,2:T(1,128)S(1)} %copy.369, s32[]{:T(128)S(6)} %copy.402, s32[]{:T(128)} %constant.102.clone.1..sunk.1, s32[]{:T(128)} %constant.102.clone.1..sunk.1, s32[]{:T(128)} %constant.102.clone.1..sunk.1, s32[]{:T(128)} %constant.102.clone.1..sunk.1) | dynamic-update-slice | bytes 3545092 | tf_op jit(solution)/shard_map/while/body/jit(dynamic_update_index_in_dim)/dynamic_update_slice | solution.py:302
  1619.5 38.1 %dynamic_update_slice.36 = f32[3,577,3,4,64]{1,0,4,3,2:T(4,128)} dynamic-update-slice(f32[3,577,3,4,64]{1,0,4,3,2:T(4,128)} %get-tuple-element.774, f32[1,577,3,4,64]{1,0,4,3,2:T(1,128)S(1)} %copy.369, s32[]{:T(128)S(6)} %copy.402, s32[]{:T(128)} %constant.102.clone.1..sunk.1, s32[]{:T(128)} %constant.102.clone.1..sunk.1, s32[]{:T(128)} %constant.102.clone.1..sunk.1, s32[]{:T(128)} %constant.102.clone.1..sunk.1) | dynamic-update-slice | bytes 3545092 | tf_op jit(solution)/shard_map/while/body/jit(dynamic_update_index_in_dim)/dynamic_update_slice | solution.py:302
  1681.3 125.5 %fusion.223 = (bf16[448,1024]{1,0:T(8,128)(2,1)}, bf16[448,1024]{1,0:T(8,128)(2,1)}) fusion(bf16[1732,1024]{1,0:T(8,128)(2,1)S(1)} %copy-done.14, bf16[1732,1024]{1,0:T(8,128)(2,1)} %pad.48), kind=kCustom, calls=%all-reduce-scatter.8 | all-reduce-scatter fusion | flops 3670017 | bytes 8929792
  1879.4 26.3 %all-reduce.30 = (bf16[2,4,64]{2,1,0:T(4,128)(2,1)S(1)}, bf16[2,4,64]{2,1,0:T(4,128)(2,1)S(1)}, bf16[16,64]{1,0:T(8,128)(2,1)S(1)}, bf16[16,64]{1,0:T(8,128)(2,1)S(1)}) all-reduce(bf16[2,4,64]{2,1,0:T(4,128)(2,1)S(1)} %pad_maximum_fusion.3, ...), channel_id=25, replica_groups=mesh['dp'=8,'tensor'=4] {'dp'}, use_global_device_ids=true, to_apply=%region_45.46.clone | all-reduce | flops 3072 | bytes 12288
  1907.4 55.8 %reduce-scatter.63.cloned.1.call-done = f32[32,4]{1,0:T(8,128)} async-done(((f32[1024,4]{1,0:T(8,128)}), f32[32,4]{1,0:T(8,128)}) %reduce-scatter.63.cloned.1.call-update) | async-done | bytes 528
  1964.6 132.8 %reduce-scatter.65.cloned.1.call-done = f32[32,8]{1,0:T(8,128)} async-done(((f32[1024,8]{1,0:T(8,128)}), f32[32,8]{1,0:T(8,128)}) %reduce-scatter.65.cloned.1.call-update) | async-done | bytes 1040
  2099.0 28.2 %reduce-scatter.55.cloned.1.call-done = bf16[128,256]{1,0:T(8,128)(2,1)} async-done(((bf16[1024,256]{1,0:T(8,128)(2,1)}), bf16[128,256]{1,0:T(8,128)(2,1)}) %reduce-scatter.55.cloned.1.call-update) | async-done | bytes 65552
  2128.9 32.9 %reduce-scatter.51.cloned.1.call-done = bf16[128,768]{1,0:T(8,128)(2,1)} async-done(((bf16[1024,768]{1,0:T(8,128)(2,1)}), bf16[128,768]{1,0:T(8,128)(2,1)}) %reduce-scatter.51.cloned.1.call-update) | async-done | bytes 196624
  2164.2 45.5 %all-gather.59.cloned.1.call-done = bf16[4,433,1024]{2,1,0:T(8,128)(2,1)} async-done(((bf16[1,433,1024]{2,1,0:T(8,128)(2,1)}), bf16[4,433,1024]{2,1,0:T(8,128)(2,1)}) %all-gather.59.cloned.1.call-update) | async-done | bytes 3547152 | tf_op jit(solution)/shard_map/all_gather | solution.py:338
  2216.4 42.6 %all-gather.69.cloned.1.call-done = bf16[4,433,1024]{2,1,0:T(8,128)(2,1)} async-done(((bf16[1,433,1024]{2,1,0:T(8,128)(2,1)}), bf16[4,433,1024]{2,1,0:T(8,128)(2,1)}) %all-gather.69.cloned.1.call-update) | async-done | bytes 3547152 | tf_op jit(solution)/shard_map/all_gather | solution.py:341
  (576 shorter events, 847.5 us)
Async XLA Ops:
  7.2 251.4 %all-gather.51.cloned.1.call-start = ((), (), s32[]{:S(2)}) async-start(), calls=%async_computation.18 | async-start | bytes 4505600 | tf_op jit(solution)/shard_map/all_gather | solution.py:109
  212.9 73.1 %all-gather.39.cloned.1.call-start = ((), (), s32[]{:S(2)}) async-start(), calls=%async_computation.12 | async-start | bytes 1769472 | tf_op jit(solution)/shard_map/all_gather | solution.py:84
  213.8 235.5 %all-gather.53.cloned.1.call-start = ((), (), s32[]{:S(2)}) async-start(), calls=%async_computation.19 | async-start | bytes 4505600 | tf_op jit(solution)/shard_map/all_gather | solution.py:109
  387.5 4.7 collective-permute-start
  399.5 80.9 %all-gather.41.cloned.1.call-start = ((), (), s32[]{:S(2)}) async-start(), calls=%async_computation.13 | async-start | bytes 2359296 | tf_op jit(solution)/shard_map/all_gather | solution.py:87
  400.5 112.1 %all-gather.43.cloned.1.call-start = ((), (), s32[]{:S(2)}) async-start(), calls=%async_computation.14 | async-start | bytes 2359296 | tf_op jit(solution)/shard_map/all_gather | solution.py:89
  401.4 233.8 %all-gather.55.cloned.1.call-start = ((), (), s32[]{:S(2)}) async-start(), calls=%async_computation.20 | async-start | bytes 4505600 | tf_op jit(solution)/shard_map/all_gather | solution.py:109
  571.5 4.7 collective-permute-start.1
  585.4 76.6 %all-gather.45.cloned.1.call-start = ((), (), s32[]{:S(2)}) async-start(), calls=%async_computation.15 | async-start | bytes 1769472 | tf_op jit(solution)/shard_map/all_gather | solution.py:84
  586.2 203.8 %all-gather.61.cloned.1.call-start = ((), (), s32[]{:S(2)}) async-start(), calls=%async_computation.23 | async-start | bytes 4505600 | tf_op jit(solution)/shard_map/all_gather | solution.py:113
  589.0 236.3 %all-gather.57.cloned.1.call-start = ((), (), s32[]{:S(2)}) async-start(), calls=%async_computation.21 | async-start | bytes 4505600 | tf_op jit(solution)/shard_map/all_gather | solution.py:109
  761.8 4.7 collective-permute-start.2
  775.6 80.9 %all-gather.47.cloned.1.call-start = ((), (), s32[]{:S(2)}) async-start(), calls=%async_computation.16 | async-start | bytes 2359296 | tf_op jit(solution)/shard_map/all_gather | solution.py:87
  776.2 111.9 %all-gather.49.cloned.1.call-start = ((), (), s32[]{:S(2)}) async-start(), calls=%async_computation.17 | async-start | bytes 2359296 | tf_op jit(solution)/shard_map/all_gather | solution.py:89
  777.0 249.7 %all-gather.63.cloned.1.call-start = ((), (), s32[]{:S(2)}) async-start(), calls=%async_computation.24 | async-start | bytes 4505600 | tf_op jit(solution)/shard_map/all_gather | solution.py:113
  956.5 4.7 collective-permute-start.4
  977.0 357.4 %all-gather.65.cloned.1.call-start = ((), (), s32[]{:S(2)}) async-start(), calls=%async_computation.25 | async-start | bytes 4505600 | tf_op jit(solution)/shard_map/all_gather | solution.py:113
  1270.1 4.7 collective-permute-start.5
  1284.7 200.9 %all-gather.67.cloned.1.call-start = ((), (), s32[]{:S(2)}) async-start(), calls=%async_computation.26 | async-start | bytes 4505600 | tf_op jit(solution)/shard_map/all_gather | solution.py:113
  1420.6 446.1 %reduce-scatter.61.cloned.1.call-start = ((), (), s32[]{:S(2)}) async-start(), calls=%async_computation.33 | async-start | bytes 2359296
  1432.7 437.6 %reduce-scatter.57.cloned.1.call-start = ((), (), s32[]{:S(2)}) async-start(), calls=%async_computation.31 | async-start | bytes 589824
  1436.9 434.4 %reduce-scatter.53.cloned.1.call-start = ((), (), s32[]{:S(2)}) async-start(), calls=%async_computation.29 | async-start | bytes 1769472
  1448.5 424.1 %reduce-scatter.59.cloned.1.call-start = ((), (), s32[]{:S(2)}) async-start(), calls=%async_computation.32 | async-start | bytes 2359296
  1461.6 412.2 %reduce-scatter.49.cloned.1.call-start = ((), (), s32[]{:S(2)}) async-start(), calls=%async_computation.11 | async-start | bytes 2359296 | tf_op jit(solution)/shard_map/reduce_scatter | solution.py:151
  1468.9 404.8 %reduce-scatter.47.cloned.1.call-start = ((), (), s32[]{:S(2)}) async-start(), calls=%async_computation.10 | async-start | bytes 2359296 | tf_op jit(solution)/shard_map/reduce_scatter | solution.py:151
  1485.5 477.7 %reduce-scatter.63.cloned.1.call-start = ((), (), s32[]{:S(2)}) async-start(), calls=%async_computation.34 | async-start | bytes 540672
  1824.4 273.0 %reduce-scatter.65.cloned.1.call-start = ((), (), s32[]{:S(2)}) async-start(), calls=%async_computation.35 | async-start | bytes 540672
  1828.6 298.6 %reduce-scatter.55.cloned.1.call-start = ((), (), s32[]{:S(2)}) async-start(), calls=%async_computation.30 | async-start | bytes 589824
  1832.8 328.9 %reduce-scatter.51.cloned.1.call-start = ((), (), s32[]{:S(2)}) async-start(), calls=%async_computation.28 | async-start | bytes 1769472
  1844.7 364.9 %all-gather.59.cloned.1.call-start = ((), (), s32[]{:S(2)}) async-start(), calls=%async_computation.22 | async-start | bytes 4505600 | tf_op jit(solution)/shard_map/all_gather | solution.py:338
  1845.7 6.7 collective-permute-start.3
  1861.0 398.1 %all-gather.69.cloned.1.call-start = ((), (), s32[]{:S(2)}) async-start(), calls=%async_computation.27 | async-start | bytes 4505600 | tf_op jit(solution)/shard_map/all_gather | solution.py:341
  (97 other events, 2386.7 us)
Sparse Core Ops, SparseCore 0:
  213.1 45.4 all-gather.50
  260.7 25.2 all-gather.38
  399.7 49.5 all-gather.52
  451.3 29.1 all-gather.40
  482.5 29.9 all-gather.42
  585.6 49.5 all-gather.54
  636.7 25.2 all-gather.44
  663.9 46.7 all-gather.60
  775.8 49.5 all-gather.56
  827.4 29.1 all-gather.46
  858.1 29.9 all-gather.48
  977.1 49.5 all-gather.62
  1284.8 49.5 all-gather.64
  1420.8 49.5 all-gather.66
  1472.5 36.0 reduce-scatter.60
  1511.2 29.9 reduce-scatter.56
  1543.4 32.2 reduce-scatter.52
  1577.9 34.3 reduce-scatter.58
  1614.6 34.6 reduce-scatter.48
  1651.5 34.6 reduce-scatter.46
  1824.6 138.5 reduce-scatter.62
  1965.4 132.0 reduce-scatter.64
  2099.7 27.3 reduce-scatter.54
  2129.3 32.3 reduce-scatter.50
  2163.6 46.0 all-gather.58
  2211.4 47.6 all-gather.68
where the time goes:
time: 2290 us; the launch traced here: 2270 us
  waiting for transfers between devices  696 us (30%)
  blocking collectives  685 us (30%)
  local copies, waits for them, and re-layouts  553 us (24%)
  matrix products  219 us (10%)
  other arithmetic  79 us (3%)
  starting transfers between devices  23.3 us (1%)
    unnamed x8, blocking collectives  456 us
    unnamed x42, waiting for transfers between devices  268 us
    dynamic_update_slice x12, local copies, waits for them, and re-layouts, shards(): lax.map(attend_back, (query_rows.reshape(image_shape), key_rows.reshape(i...  241 us
    unnamed x250, local copies, waits for them, and re-layouts  139 us
    all_gather x4, waiting for transfers between devices, gather_cotangent(): return lax.all_gather(token_rows, 'tensor', axis=0, tiled=True)[:group_rows]  99.3 us
    all_gather x4, waiting for transfers between devices, spread_rows(): return lax.all_gather(token_rows, 'tensor', axis=0, tiled=True)[:group_rows]  93.6 us
    all_gather x1, blocking collectives, shards(): lax.all_gather(tok_bias, ('dp', 'tensor'), axis=2, tiled=True)  75.6 us
    all_gather x1, blocking collectives, shards(): lax.all_gather(ln_gain, ('dp', 'tensor'), axis=2, tiled=True)  69.4 us
  transfers between devices with their start and end apart: 34, of which 26 were waited for; matrix products, arithmetic and copies ran while one was open for 27% of the time, Pallas kernels for 0%

commit v1 on v0

--- a/solution.py
+++ b/solution.py
@@ -1,6 +1,11 @@
 import jax
 import jax.numpy as jnp
+import numpy as np
 from jax import lax
+from jax.experimental import pallas as pl
+from jax.experimental.layout import Layout, with_layout_constraint
+from jax.experimental.pallas import tpu as pltpu
+from jax.sharding import Mesh
 from jax.sharding import PartitionSpec as P
 
 HEAD_DIM = 64
@@ -360,29 +365,804 @@
     )
 
 
+CELLS = ("z", "core", "y", "x")
+PHASES = {
+    (1, 4): (("mlp", 1),),
+    (0, 1): (("att", 1),),
+    (0, 4): (("att", 1), ("mlp", 1)),
+    (0, 5): (("mlp", 0),),
+}
+FLIP = ((0, 1), (1, 0))
+TILE = 16
+LANES = 128
+NEGATIVE = -1e30
+VMEM_LIMIT = 56 * 1024 * 1024
+
+
+def round_up(count, multiple):
+    return (count + multiple - 1) // multiple * multiple
+
+
+WHOLE = round_up(SEQ, TILE)
+PART_ROWS = (SEQ + 1) // 2
+PART = round_up(PART_ROWS, TILE)
+CHIP_ROWS = WHOLE + PART
+SHARE = CHIP_ROWS // 2
+SPILL = WHOLE - SHARE
+NT = (((1,), (1,)), ((), ()))
+TN = (((0,), (0,)), ((), ()))
+NN = (((1,), (0,)), ((), ()))
+
+
+def product(left, right, dims):
+    return lax.dot_general(left, right, dims, preferred_element_type=jnp.float32)
+
+
+def lane_pick(values, half):
+    lane = lax.broadcasted_iota(jnp.int32, (1, values.shape[1]), 1)
+    keep = lane < HEAD_DIM if half == 0 else lane >= HEAD_DIM
+    return jnp.where(keep, values, jnp.zeros_like(values))
+
+
+def whole_rows(ref, core):
+    first = pl.multiple_of(core * SHARE, TILE)
+    second = pl.multiple_of((1 - core) * SHARE, TILE)
+    return jnp.concatenate([ref[pl.ds(first, SHARE), :], ref[pl.ds(second, SPILL), :]], axis=0)
+
+
+def store_whole(ref, core, values, lanes):
+    first = pl.multiple_of(core * SHARE, TILE)
+    second = pl.multiple_of((1 - core) * SHARE, TILE)
+    ref[pl.ds(first, SHARE), lanes] = values[:SHARE]
+    ref[pl.ds(second, SPILL), lanes] = values[SHARE:]
+
+
+def part_rows(ref, core):
+    start = pl.multiple_of((1 - core) * SHARE + SPILL, TILE)
+    return ref[pl.ds(start, PART), :]
+
+
+def whole_keys():
+    return lax.broadcasted_iota(jnp.int32, (WHOLE, 1), 0) < SEQ
+
+
+def part_keys(mine):
+    row = lax.broadcasted_iota(jnp.int32, (2 * PART, 1), 0)
+    return (row < mine) | ((row >= PART) & (row < PART + SEQ - mine))
+
+
+def attend_pair(query, key, value, good, lse_ref, slot):
+    total = None
+    for half in range(2):
+        scores = product(lane_pick(key, half), query, NT)
+        scores = jnp.where(good, scores, NEGATIVE)
+        peak = jnp.max(scores, axis=0, keepdims=True)
+        exponent = jnp.exp(scores - peak)
+        sums = jnp.sum(exponent, axis=0, keepdims=True)
+        probs = (exponent * (1.0 / sums)).astype(jnp.bfloat16)
+        lse_ref[0, pl.ds(2 * slot + half, 1), :] = peak + jnp.log(sums)
+        mixed = product(lane_pick(value, half), probs, TN)
+        total = mixed if total is None else total + mixed
+    return total.T.astype(jnp.bfloat16)
+
+
+def attend_whole_kernel(place, qkv_a, qkv_b, mix_a, mix_b, lse_ref):
+    core = place[0]
+    good = whole_keys()
+    for slot, (qkv, mix) in enumerate(((qkv_a, mix_a), (qkv_b, mix_b))):
+        rows = whole_rows(qkv, core)
+        mixed = attend_pair(
+            rows[:, :LANES], rows[:, LANES : 2 * LANES], rows[:, 2 * LANES :], good, lse_ref, slot
+        )
+        store_whole(mix, core, mixed, slice(None))
+
+
+def attend_part_kernel(place, qkv_a, qkv_b, far_a, far_b, mix_a, mix_b, lse_ref):
+    core = place[0]
+    good = part_keys(place[1])
+    for slot, (qkv, far, mix) in enumerate(((qkv_a, far_a, mix_a), (qkv_b, far_b, mix_b))):
+        rows = part_rows(qkv, core)
+        key = jnp.concatenate([rows[:, LANES : 2 * LANES], far[:, :LANES]], axis=0)
+        value = jnp.concatenate([rows[:, 2 * LANES :], far[:, LANES:]], axis=0)
+        mix[...] = attend_pair(rows[:, :LANES], key, value, good, lse_ref, slot)
+
+
+def attend_pair_back(query, key, value, upstream, good, lse_ref, slot):
+    grad_key = grad_value = grad_query = None
+    for half in range(2):
+        lse = lse_ref[0, pl.ds(2 * slot + half, 1), :]
+        key_half = lane_pick(key, half)
+        scores = product(key_half, query, NT)
+        probs = jnp.where(good, jnp.exp(scores - lse), 0.0)
+        grad_probs = product(lane_pick(value, half), upstream, NT)
+        inner = jnp.sum(probs * grad_probs, axis=0, keepdims=True)
+        grad_scores = (probs * (grad_probs - inner)).astype(jnp.bfloat16)
+        probs = probs.astype(jnp.bfloat16)
+        some_key = product(grad_scores, lane_pick(query, half), NN)
+        some_value = product(probs, lane_pick(upstream, half), NN)
+        some_query = product(key_half, grad_scores, TN)
+        grad_key = some_key if grad_key is None else grad_key + some_key
+        grad_value = some_value if grad_value is None else grad_value + some_value
+        grad_query = some_query if grad_query is None else grad_query + some_query
+    return grad_query.T * HEAD_DIM ** (-0.5), grad_key, grad_value
+
+
+def store_sums(sum_ref, slot, grad_query, grad_value):
+    sum_ref[0, pl.ds(2 * slot, 1), :] = jnp.sum(grad_query, axis=0, keepdims=True)
+    sum_ref[0, pl.ds(2 * slot + 1, 1), :] = jnp.sum(grad_value, axis=0, keepdims=True)
+
+
+def back_whole_kernel(place, qkv_a, qkv_b, up_a, up_b, lse_ref, out_a, out_b, sum_ref):
+    core = place[0]
+    good = whole_keys()
+    for slot, (qkv, up, out) in enumerate(((qkv_a, up_a, out_a), (qkv_b, up_b, out_b))):
+        rows = whole_rows(qkv, core)
+        grads = attend_pair_back(
+            rows[:, :LANES],
+            rows[:, LANES : 2 * LANES],
+            rows[:, 2 * LANES :],
+            whole_rows(up, core),
+            good,
+            lse_ref,
+            slot,
+        )
+        store_sums(sum_ref, slot, grads[0], grads[2])
+        for place_of, grad in enumerate(grads):
+            lanes = slice(place_of * LANES, (place_of + 1) * LANES)
+            store_whole(out, core, grad.astype(jnp.bfloat16), lanes)
+
+
+def back_part_kernel(
+    place, qkv_a, qkv_b, far_a, far_b, up_a, up_b, lse_ref, own_a, own_b, out_a, out_b, sum_ref
+):
+    core = place[0]
+    good = part_keys(place[1])
+    groups = ((qkv_a, far_a, up_a, own_a, out_a), (qkv_b, far_b, up_b, own_b, out_b))
+    for slot, (qkv, far, up, own, out) in enumerate(groups):
+        rows = part_rows(qkv, core)
+        key = jnp.concatenate([rows[:, LANES : 2 * LANES], far[:, :LANES]], axis=0)
+        value = jnp.concatenate([rows[:, 2 * LANES :], far[:, LANES:]], axis=0)
+        grad_query, grad_key, grad_value = attend_pair_back(
+            rows[:, :LANES], key, value, part_rows(up, core), good, lse_ref, slot
+        )
+        store_sums(sum_ref, slot, grad_query, grad_value)
+        own[:, :LANES] = grad_query
+        own[:, LANES : 2 * LANES] = grad_key[:PART]
+        own[:, 2 * LANES :] = grad_value[:PART]
+        out[:, :LANES] = grad_key[PART:].astype(jnp.bfloat16)
+        out[:, LANES:] = grad_value[PART:].astype(jnp.bfloat16)
+
+
+def by_pair(rows, lanes):
+    return pl.BlockSpec((rows, lanes), lambda pair: (0, pair))
+
+
+def stats(rows):
+    return pl.BlockSpec((1, 8, rows), lambda pair: (pair, 0, 0))
+
+
+def kernel_call(kernel, pairs, ins, in_specs, outs, out_specs):
+    return pl.pallas_call(
+        kernel,
+        grid=(pairs,),
+        in_specs=[pl.BlockSpec(memory_space=pltpu.SMEM)] + in_specs,
+        out_specs=out_specs,
+        out_shape=[jax.ShapeDtypeStruct(shape, kind) for shape, kind in outs],
+        compiler_params=pltpu.CompilerParams(
+            dimension_semantics=("arbitrary",), vmem_limit_bytes=VMEM_LIMIT
+        ),
+    )(*ins)
+
+
+def attend_whole(place, qkv, pairs):
+    mix = ((CHIP_ROWS, pairs * LANES), jnp.bfloat16)
+    *mixed, lse = kernel_call(
+        attend_whole_kernel,
+        pairs,
+        (place, *qkv),
+        [by_pair(CHIP_ROWS, 3 * LANES)] * 2,
+        [mix, mix, ((pairs, 8, WHOLE), jnp.float32)],
+        [by_pair(CHIP_ROWS, LANES)] * 2 + [stats(WHOLE)],
+    )
+    return mixed, lse
+
+
+def attend_part(place, qkv, far, pairs):
+    mix = ((PART, pairs * LANES), jnp.bfloat16)
+    *mixed, lse = kernel_call(
+        attend_part_kernel,
+        pairs,
+        (place, *qkv, *far),
+        [by_pair(CHIP_ROWS, 3 * LANES)] * 2 + [by_pair(PART, 2 * LANES)] * 2,
+        [mix, mix, ((pairs, 8, PART), jnp.float32)],
+        [by_pair(PART, LANES)] * 2 + [stats(PART)],
+    )
+    return mixed, lse
+
+
+def back_whole(place, qkv, upstream, lse, pairs):
+    out = ((CHIP_ROWS, 3 * pairs * LANES), jnp.bfloat16)
+    *grads, sums = kernel_call(
+        back_whole_kernel,
+        pairs,
+        (place, *qkv, *upstream, lse),
+        [by_pair(CHIP_ROWS, 3 * LANES)] * 2
+        + [by_pair(CHIP_ROWS, LANES)] * 2
+        + [stats(WHOLE)],
+        [out, out, ((pairs, 8, LANES), jnp.float32)],
+        [by_pair(CHIP_ROWS, 3 * LANES)] * 2 + [stats(LANES)],
+    )
+    return grads, sums
+
+
+def back_part(place, qkv, far, upstream, lse, pairs):
+    own = ((PART, 3 * pairs * LANES), jnp.float32)
+    out = ((PART, 2 * pairs * LANES), jnp.bfloat16)
+    own_a, own_b, out_a, out_b, sums = kernel_call(
+        back_part_kernel,
+        pairs,
+        (place, *qkv, *far, *upstream, lse),
+        [by_pair(CHIP_ROWS, 3 * LANES)] * 2
+        + [by_pair(PART, 2 * LANES)] * 2
+        + [by_pair(CHIP_ROWS, LANES)] * 2
+        + [stats(PART)],
+        [own, own, out, out, ((pairs, 8, LANES), jnp.float32)],
+        [by_pair(PART, 3 * LANES)] * 2 + [by_pair(PART, 2 * LANES)] * 2 + [stats(LANES)],
+    )
+    return (own_a, own_b), (out_a, out_b), sums
+
+
+def give_kernel(place, round_00, round_01, round_10, round_11, out):
+    y, x = place[2], place[3]
+    near = [jnp.where(x == 0, a, b) for a, b in ((round_00[...], round_10[...]), (round_01[...], round_11[...]))]
+    far = [jnp.where(x == 1, a, b) for a, b in ((round_00[...], round_10[...]), (round_01[...], round_11[...]))]
+    row = 0
+    tails = []
+    for rounds in (near, far):
+        whole = jnp.where(y == 0, rounds[0], rounds[1]).astype(jnp.float32)
+        tail = jnp.where(y == 1, rounds[0], rounds[1]).astype(jnp.float32)
+        out[row : row + SHARE, :] = whole
+        out[row + SHARE : row + SEQ, :] = tail[: SEQ - SHARE]
+        tails.append(tail)
+        row += SEQ
+    rest = SEQ - PART_ROWS
+    out[row : row + PART_ROWS, :] = tails[0][SPILL : SPILL + PART_ROWS]
+    out[row + PART_ROWS : row + SEQ, :] = tails[1][SPILL : SPILL + rest]
+
+
+def give_call(place, rounds):
+    width = rounds[0].shape[1]
+    wide = 2 * LANES
+    grid_spec = pltpu.PrefetchScalarGridSpec(
+        num_scalar_prefetch=1,
+        grid=(width // wide,),
+        in_specs=[pl.BlockSpec((SHARE, wide), lambda col, place: (0, col))] * 4,
+        out_specs=pl.BlockSpec((3 * SEQ, wide), lambda col, place: (0, col)),
+    )
+    return pl.pallas_call(
+        give_kernel,
+        grid_spec=grid_spec,
+        out_shape=jax.ShapeDtypeStruct((3 * SEQ, width), jnp.float32),
+        compiler_params=pltpu.CompilerParams(vmem_limit_bytes=VMEM_LIMIT),
+        name="give_rows",
+    )(place, *rounds)
+
+
+def natural(values):
+    return with_layout_constraint(values, Layout((0, 1)))
+
+
+def tie(*values):
+    return lax.optimization_barrier(values)
+
+
+def cell_moves(sizes, target):
+    moves = []
+    index = {cell: number for number, cell in enumerate(np.ndindex(*sizes))}
+    for cell, number in index.items():
+        goal = target(*cell)
+        if goal is not None:
+            moves.append((number, index[goal]))
+    return moves
+
+
+def cells_body(sizes):
+    n_z, _, _, _ = sizes
+    trade = cell_moves(
+        sizes, lambda z, c, y, x: (z, c, y, 1 - x) if c == 0 else (z, c, 1 - y, x)
+    )
+    relay_y = cell_moves(
+        sizes, lambda z, c, y, x: (z, 1, 1 - y, x) if c == 0 else (z, 0, y, x)
+    )
+    relay_x = cell_moves(sizes, lambda z, c, y, x: (z, 1, y, 1 - x) if c == 1 else None)
+    back_y = cell_moves(
+        sizes, lambda z, c, y, x: (z, 0, 1 - y, x) if c == 1 else (z, 1, y, x)
+    )
+    lend = cell_moves(
+        sizes, lambda z, c, y, x: (z, c, 1 - y, x) if c == y else (z, 1 - c, y, x)
+    )
+    repay = cell_moves(
+        sizes, lambda z, c, y, x: (z, c, 1 - y, x) if c != y else (z, 1 - c, y, x)
+    )
+    images_axis = ("z", "core")
+    chips = ("y", "x")
+
+    def move(values, moves):
+        return lax.ppermute(values, CELLS, moves)
+
+    def spread(quarter, core):
+        half = quarter.shape[0] // 2
+        slot_a = move(quarter, trade)
+        upper = move(slot_a[:half], relay_y)
+        lower = move(slot_a[half:], relay_x)
+        slot_b = jnp.where(core == 0, quarter, jnp.concatenate([upper, lower], axis=0))
+        return slot_a, natural(slot_b)
+
+    def collect_far(grad_b):
+        half = grad_b.shape[0] // 2
+        return (move(grad_b[:half], back_y), move(grad_b[half:], relay_x))
+
+    def collect_near(grad_a, come, core):
+        half = grad_a.shape[0] // 2
+        come = jnp.where(core == 0, come[0], come[1])
+        piece = lax.dynamic_slice(grad_a, (core * half, 0), come.shape)
+        piece = (piece.astype(jnp.float32) + come.astype(jnp.float32)).astype(jnp.bfloat16)
+        grad_a = lax.dynamic_update_slice(grad_a, piece, (core * half, 0))
+        return move(grad_a, trade)
+
+    def collect_end(grad_b, traded, home):
+        if isinstance(grad_b, list):
+            mine = [
+                jnp.where(home, kept.astype(jnp.float32) + come.astype(jnp.float32), 0.0)
+                for kept, come in zip(grad_b, traded)
+            ]
+            mine = jnp.concatenate([part.astype(jnp.bfloat16) for part in mine], axis=1)
+        else:
+            kept = jnp.where(home, grad_b.astype(jnp.float32), 0.0)
+            mine = (kept + traded.astype(jnp.float32)).astype(jnp.bfloat16)
+        return natural(mine)
+
+    def collect_sum(mine):
+        return lax.psum_scatter(mine, images_axis, scatter_dimension=0, tiled=True)
+
+    def start_stream(grads, pack):
+        return {"grads": grads, "pack": pack, "held": collect_far(grads[1]), "step": 0}
+
+    def start_pair(grads, home, pack):
+        held = [move(grad, repay) for grad in grads]
+        return {"grads": (None, grads), "pack": pack, "held": held, "step": 1, "home": home}
+
+    def advance(value, stream, core):
+        value, held = tie(value, stream["held"])
+        step = stream["step"]
+        if step == 0:
+            held = collect_near(stream["grads"][0], held, core)
+        elif step == 1:
+            home = stream.get("home", core == 0)
+            value, held = tie(value, collect_end(stream["grads"][1], held, home))
+            held = collect_sum(held)
+        stream["held"], stream["step"] = held, step + 1
+        return value
+
+    def gather_quad(values):
+        across = lax.ppermute(values, "x", FLIP)
+        near = flip(values)
+        far = flip(across)
+        return jnp.concatenate([values, near, across, far], axis=0)
+
+    def reduce_quad(left, right, dims):
+        far = product(left[3 * SHARE :], right, dims).astype(jnp.bfloat16)
+        far = flip(far)
+        across = product(left[2 * SHARE : 3 * SHARE], right, dims)
+        across = (across + far.astype(jnp.float32)).astype(jnp.bfloat16)
+        across = lax.ppermute(across, "x", FLIP)
+        near = product(left[SHARE : 2 * SHARE], right, dims).astype(jnp.bfloat16)
+        near = flip(near)
+        own = product(left[:SHARE], right, dims)
+        return own + near.astype(jnp.float32) + across.astype(jnp.float32)
+
+    def total_of(table):
+        for axis in ("x", "y", "core"):
+            come = lax.ppermute(table, axis, FLIP)
+            table = table + come
+        gap = 1
+        while gap < n_z:
+            if n_z % (2 * gap):
+                return lax.psum(table, "z")
+            partner = [(z, z ^ gap) for z in range(n_z)]
+            table = table + lax.ppermute(table, "z", partner)
+            gap *= 2
+        return table
+
+    def flip(values):
+        return lax.ppermute(values, "core", FLIP)
+
+    def both(values):
+        return jnp.concatenate([values, flip(values)], axis=0)
+
+    def reduce_pair(lefts, rights, dims):
+        other = sum(
+            product(left[SHARE:], right, dims) for left, right in zip(lefts, rights)
+        )
+        other = flip(other.astype(jnp.bfloat16))
+        own = sum(product(left[:SHARE], right, dims) for left, right in zip(lefts, rights))
+        return own + other.astype(jnp.float32)
+
+    def share_of(rows, x, part):
+        width = rows.shape[1]
+        if part == 0:
+            return lax.dynamic_slice(rows, (SEQ * x, 0), (SHARE, width))
+        tail = lax.dynamic_slice(rows, (SEQ * x + SHARE, 0), (SEQ - SHARE, width))
+        split = lax.dynamic_slice(
+            rows, (2 * SEQ + PART_ROWS * x, 0), (SEQ - PART_ROWS, width)
+        )
+        last = rows[2 * SEQ + PART_ROWS - 1 : 2 * SEQ + PART_ROWS]
+        last = jnp.where(x == 0, last, jnp.zeros_like(last))
+        return jnp.concatenate(
+            [
+                tail,
+                jnp.zeros((WHOLE - SEQ, width), rows.dtype),
+                split,
+                last,
+                jnp.zeros((PART - PART_ROWS, width), rows.dtype),
+            ],
+            axis=0,
+        )
+
+    def take_share(rows, core, y, x):
+        shares = share_of(rows, x, 0), share_of(rows, x, 1)
+        own = jnp.where(core == 0, shares[0], shares[1])
+        come = flip(jnp.where(core == 0, shares[1], shares[0]))
+        return jnp.where(core == y, own, come)
+
+    def share_rows(share, home):
+        share = share.astype(jnp.bfloat16)
+        rounds = []
+        for number in range(4):
+            dx, dc = divmod(number, 2)
+            moves = cell_moves(
+                sizes, lambda z, c, y, x, dx=dx, dc=dc: (z, y, c ^ dc, x ^ dx)
+            )
+            moves = [(a, b) for a, b in moves if a != b]
+            come = move(share, moves)
+            rounds.append(jnp.where(home, share, come) if number == 0 else come)
+        return rounds
+
+    def cells_step(inputs, grad_out, w_qkv, b_qv, w_out, w_up, b_up, w_down, ln_gain, tok_bias):
+        core, y, x = (lax.axis_index(name) for name in ("core", "y", "x"))
+        quarter_a = jnp.where(core == 0, 2 * y + 1 - x, 2 * (1 - y) + x)
+        quarter_b = jnp.where(core == 0, 2 * y + x, 2 * (1 - y) + 1 - x)
+        quarters = (quarter_a, quarter_b)
+        place = jnp.stack([core, PART_ROWS - x, y, x]).astype(jnp.int32)
+        width = inputs.shape[1]
+        heads = b_qv.shape[2]
+        local = heads * HEAD_DIM
+        pairs = local // LANES
+        units = w_up.shape[2]
+        n_dp = 2 * n_z
+        n_dev = 4 * n_dp
+        piece = width // n_dev
+
+        def pack_attention(layer):
+            cols = [
+                w_qkv[layer, member][:, pair * LANES : (pair + 1) * LANES]
+                for pair in range(pairs)
+                for member in range(3)
+            ]
+            return jnp.concatenate(cols + [w_out[layer].T], axis=1)
+
+        packs = []
+        for layer in range(LAYERS):
+            packs += [pack_attention(layer), w_up[layer], w_down[layer].T]
+        whole = []
+        for pack in packs:
+            whole.append(natural(lax.all_gather(natural(pack), images_axis, axis=0, tiled=True)))
+        home = core == y
+        weights = []
+        for pack, quarter in enumerate(whole):
+            if pack % 3 == 0:
+                weights.append(spread(quarter, core))
+            else:
+                weights.append((quarter, move(quarter, lend)))
+
+        small = jnp.concatenate(
+            [
+                ln_gain.reshape(-1, piece),
+                tok_bias.reshape(-1, piece),
+                b_qv.astype(jnp.float32).reshape(-1, piece),
+                b_up.astype(jnp.float32).reshape(-1, piece),
+            ],
+            axis=0,
+        )
+        n_gain, n_bias, n_qv = 2 * LAYERS, 4 * LAYERS, b_qv.size // piece
+        table = lax.all_gather(small, images_axis, axis=0)
+        table = lax.all_gather(table, chips, axis=0)
+        inputs, grad_out, table, _ = tie(inputs, grad_out, table, whole[0])
+        stream = take_share(inputs, core, y, x)
+        cotangent = take_share(grad_out, core, y, x)
+        stream, cotangent = tie(stream, cotangent)
+        first_rows = gather_quad(cotangent.astype(jnp.bfloat16))
+        tokens = jnp.transpose(table[:, :, : n_gain + n_bias], (2, 1, 0, 3)).reshape(-1, width)
+        gains = tokens[:n_gain].reshape(LAYERS, 2, width)
+        shifts = tokens[n_gain:].reshape(LAYERS, 4, width)
+        f_head = b_qv.shape[3]
+        rows_up, f_up = b_up.shape[1], b_up.shape[2]
+        head_bias = []
+        for quarter in quarters:
+            mine = lax.dynamic_index_in_dim(table, quarter, 0, keepdims=False)
+            part = mine[:, n_gain + n_bias : n_gain + n_bias + n_qv]
+            part = part.reshape(n_dp, LAYERS, 2, heads, f_head)
+            head_bias.append(jnp.transpose(part, (1, 2, 3, 0, 4)).reshape(LAYERS, 2, local))
+        up_quarter = 2 * core + x
+        mine = lax.dynamic_index_in_dim(table, up_quarter, 0, keepdims=False)
+        part = mine[:, n_gain + n_bias + n_qv :].reshape(n_dp, LAYERS, rows_up, f_up)
+        up_bias = jnp.transpose(part, (1, 2, 0, 3)).reshape(LAYERS, 1, units)
+
+        def qkv_bias(slot, layer):
+            rows = head_bias[slot][layer].reshape(2, pairs, LANES)
+            zero = jnp.zeros_like(rows[0])
+            return jnp.stack([rows[0], zero, rows[1]], axis=1).reshape(1, -1)
+
+        unit = jnp.ones((LANES,), jnp.float32)
+        qkv_scale = jnp.tile(jnp.concatenate([unit * HEAD_DIM ** (-0.5), unit, unit]), pairs)
+        part_start = jnp.where(core == 0, SHARE + SPILL, SPILL)
+
+        def exchange_part(values):
+            swapped = jnp.concatenate([values[1], values[0]], axis=1)
+            come = lax.ppermute(swapped, "x", FLIP)
+            return jnp.split(come, 2, axis=1)
+
+        def lent(pack, value):
+            quarter, come = weights[pack]
+            value, come = tie(value, come)
+            weights[pack] = natural(jnp.where(home, quarter, come))
+            return value
+
+        saved_list = []
+        for layer in range(LAYERS):
+            att_w = weights[3 * layer]
+            out_w = [slot[:, 3 * local :] for slot in att_w]
+            normed_one, hat_one, inv_one = norm_forward(
+                stream, gains[layer, 0], shifts[layer, 0]
+            )
+            rows_one = both(normed_one.astype(jnp.bfloat16))
+            biases = [qkv_bias(slot, layer) for slot in range(2)]
+            qkv = [
+                (
+                    (product(rows_one, att_w[slot][:, : 3 * local], NN) + biases[slot])
+                    * qkv_scale
+                ).astype(jnp.bfloat16)
+                for slot in range(2)
+            ]
+            halves = []
+            for slot in range(2):
+                rows = lax.dynamic_slice(qkv[slot], (part_start, 0), (PART, 3 * local))
+                rows = rows.reshape(PART, pairs, 3 * LANES)[:, :, LANES:]
+                halves.append(rows.reshape(PART, 2 * local))
+            far = exchange_part(halves)
+            mixed, lse_whole = attend_whole(place, qkv, pairs)
+            far, mixed = tie(far, mixed)
+            mixed_part, lse_part = attend_part(place, qkv, far, pairs)
+            mixed = [
+                lax.dynamic_update_slice(rows, part, (part_start, 0))
+                for rows, part in zip(mixed, mixed_part)
+            ]
+            middle = stream + reduce_pair(mixed, out_w, NT) + shifts[layer, 1]
+            normed_two, hat_two, inv_two = norm_forward(
+                middle, gains[layer, 1], shifts[layer, 2]
+            )
+            rows_two = gather_quad(normed_two.astype(jnp.bfloat16))
+            rows_two = lent(3 * layer + 1, rows_two)
+            up_w = weights[3 * layer + 1]
+            hidden = product(rows_two, up_w, NN) + up_bias[layer]
+            activation = gelu_value(hidden).astype(jnp.bfloat16)
+            if layer == LAYERS - 1:
+                slope = gelu_slope(hidden).astype(jnp.bfloat16)
+            else:
+                (slope,) = tie(gelu_slope(tie(hidden)[0]).astype(jnp.bfloat16))
+            activation = lent(3 * layer + 2, activation)
+            down_w = weights[3 * layer + 2]
+            if layer < LAYERS - 1:
+                stream = middle + reduce_quad(activation, down_w, NT)
+                stream = stream + shifts[layer, 3]
+            saved_list.append(
+                (
+                    rows_one,
+                    hat_one,
+                    inv_one,
+                    qkv,
+                    far,
+                    lse_whole,
+                    lse_part,
+                    mixed,
+                    rows_two,
+                    hat_two,
+                    inv_two,
+                    slope,
+                    activation,
+                )
+            )
+        token_grads, head_grads, unit_grads = ([None] * LAYERS for _ in range(3))
+        streams = {}
+
+        def advance_all(value, layer, phase):
+            for stream in PHASES.get((layer, phase), ()):
+                value = advance(value, streams[stream], core)
+            return value
+
+        for layer in reversed(range(LAYERS)):
+            (
+                rows_one,
+                hat_one,
+                inv_one,
+                qkv,
+                far,
+                lse_whole,
+                lse_part,
+                mixed,
+                rows_two,
+                hat_two,
+                inv_two,
+                slope,
+                activation,
+            ) = saved_list[layer]
+            att_w, up_w, down_w = weights[3 * layer : 3 * layer + 3]
+            out_w = [slot[:, 3 * local :] for slot in att_w]
+            shift_down = jnp.sum(cotangent, axis=0)
+            if layer == LAYERS - 1:
+                cot_rows = first_rows
+            else:
+                cot_rows = gather_quad(cotangent.astype(jnp.bfloat16))
+            grad_hidden = product(cot_rows, down_w, NN) * slope.astype(jnp.float32)
+            unit_grads[layer] = jnp.sum(grad_hidden, axis=0)
+            hidden_rows = grad_hidden.astype(jnp.bfloat16)
+            hidden_rows = advance_all(hidden_rows, layer, 0)
+            back_two = reduce_quad(hidden_rows, up_w, NT)
+            grad_down = natural(product(cot_rows, activation, TN).astype(jnp.bfloat16))
+            grad_up = natural(product(rows_two, hidden_rows, TN).astype(jnp.bfloat16))
+            streams["mlp", layer] = start_pair([grad_up, grad_down], home, 3 * layer + 1)
+            back_two = advance_all(back_two, layer, 1)
+            if layer == LAYERS - 1:
+                back_two, last = tie(back_two, activation)
+                stream = middle + reduce_quad(last, down_w, NT)
+                every_out = share_rows(stream + shifts[layer, 3], home)
+            dstream, gain_two, shift_two = norm_backward(
+                back_two, gains[layer, 1], hat_two, inv_two
+            )
+            cotangent = cotangent + dstream
+            shift_out = jnp.sum(cotangent, axis=0)
+            cot_rows = both(cotangent.astype(jnp.bfloat16))
+            grad_mixed = [
+                product(cot_rows, out_w[slot], NN).astype(jnp.bfloat16) for slot in range(2)
+            ]
+            grad_out_w = [
+                product(cot_rows, mixed[slot], TN).astype(jnp.bfloat16) for slot in range(2)
+            ]
+            grad_mixed = advance_all(grad_mixed, layer, 2)
+            own_part, far_part, part_sums = back_part(place, qkv, far, grad_mixed, lse_part, pairs)
+            grad_mixed, far_part = tie(grad_mixed, far_part)
+            grad_mixed = advance_all(grad_mixed, layer, 3)
+            come_part = exchange_part(far_part)
+            grad_qkv, whole_sums = back_whole(place, qkv, grad_mixed, lse_whole, pairs)
+            grad_qkv = advance_all(grad_qkv, layer, 4)
+            sums = (part_sums + whole_sums)[:, :4].reshape(pairs, 2, 2, LANES)
+            head_grads[layer] = [
+                jnp.transpose(sums[:, slot], (1, 0, 2)).reshape(2, local) for slot in range(2)
+            ]
+            for slot in range(2):
+                come = come_part[slot].astype(jnp.float32).reshape(PART, pairs, 2 * LANES)
+                come = jnp.pad(come, ((0, 0), (0, 0), (LANES, 0))).reshape(PART, 3 * local)
+                part = (own_part[slot] + come).astype(jnp.bfloat16)
+                grad_qkv[slot] = lax.dynamic_update_slice(grad_qkv[slot], part, (part_start, 0))
+            grad_att = [
+                product(rows_one, grad_qkv[slot], TN).astype(jnp.bfloat16)
+                for slot in range(2)
+            ]
+            grad_att = [
+                natural(jnp.concatenate([grad_att[slot], grad_out_w[slot]], axis=1))
+                for slot in range(2)
+            ]
+            streams["att", layer] = start_stream(grad_att, 3 * layer)
+            qkv_w = [slot[:, : 3 * local] for slot in att_w]
+            back_one = reduce_pair(grad_qkv, qkv_w, NT)
+            back_one = advance_all(back_one, layer, 5)
+            dstream, gain_one, shift_one = norm_backward(
+                back_one, gains[layer, 0], hat_one, inv_one
+            )
+            cotangent = cotangent + dstream
+            token_grads[layer] = (
+                [gain_one, gain_two],
+                [shift_one, shift_out, shift_two, shift_down],
+            )
+        cotangent = advance(cotangent, streams["att", 0], core)
+        every_back = share_rows(cotangent, home)
+        rows = [row for layer in range(LAYERS) for row in token_grads[layer][0]]
+        rows += [row for layer in range(LAYERS) for row in token_grads[layer][1]]
+        spots = [lax.broadcasted_iota(jnp.int32, (4, 1), 0) == quarter for quarter in quarters]
+        for layer in range(LAYERS):
+            for member in range(2):
+                parts = [
+                    jnp.where(spots[slot], head_grads[layer][slot][member][None], 0.0)
+                    for slot in range(2)
+                ]
+                rows.append((parts[0] + parts[1]).reshape(-1))
+        table = [jnp.stack(rows)]
+        for layer in range(LAYERS):
+            spot = lax.broadcasted_iota(jnp.int32, (4, 1), 0) == up_quarter
+            table.append(jnp.where(spot, unit_grads[layer][None], 0.0))
+        table = total_of(jnp.concatenate(table, axis=0))
+        table = advance(table, streams["att", 0], core)
+        for stream in streams.values():
+            while stream["step"] < 3:
+                advance((), stream, core)
+        full_out = give_call(place, every_out)
+        full_back = give_call(place, every_back)
+        z = lax.axis_index("z")
+        spot = 2 * z + core
+        column = (4 * spot + 2 * y + x) * piece
+        mine = lax.dynamic_slice(table, (0, column), (n_gain + n_bias, piece))
+        grad_gain = mine[:n_gain].reshape(LAYERS, 2, piece)
+        grad_shift = mine[n_gain:].reshape(LAYERS, 4, piece)
+        base = n_gain + n_bias
+        mine = table[base : base + 2 * LAYERS].reshape(2 * LAYERS, 4, heads, HEAD_DIM)
+        mine = lax.dynamic_index_in_dim(mine, 2 * y + x, 1, keepdims=False)
+        mine = lax.dynamic_slice_in_dim(mine, spot * f_head, f_head, 2)
+        grad_qv = mine.reshape(b_qv.shape)
+        mine = table[base + 2 * LAYERS :].reshape(LAYERS, 4, rows_up, -1)
+        mine = lax.dynamic_index_in_dim(mine, 2 * y + x, 1, keepdims=False)
+        grad_upb = lax.dynamic_slice_in_dim(mine, spot * f_up, f_up, 2)
+        ended = {
+            kind: [streams[kind, layer]["held"].astype(jnp.float32) for layer in range(LAYERS)]
+            for kind in ("att", "mlp")
+        }
+
+        def unpack(grad):
+            cols = grad[:, : 3 * local].reshape(-1, pairs, 3, LANES)
+            return jnp.transpose(cols, (2, 0, 1, 3)).reshape(3, -1, local)
+
+        return (
+            full_out,
+            full_back,
+            jnp.stack([unpack(grad) for grad in ended["att"]]),
+            grad_qv,
+            jnp.stack([grad[:, 3 * local :].T for grad in ended["att"]]),
+            jnp.stack([grad[:, :units] for grad in ended["mlp"]]),
+            grad_upb,
+            jnp.stack([grad[:, units:].T for grad in ended["mlp"]]),
+            grad_gain,
+            grad_shift,
+        )
+
+    return cells_step
+
+
+def specs_for(images, group):
+    both_axes = (*images, *group)
+    rows = (
+        P(images, None),
+        P(images, None),
+    )
+    rest = (
+        P(None, None, images, group),
+        P(None, None, group, images),
+        P(None, group, images),
+        P(None, images, group),
+        P(None, group, images),
+        P(None, group, images),
+        P(None, None, both_axes),
+        P(None, None, both_axes),
+    )
+    return rows + rest
+
+
 def solution(mesh):
-    in_specs = (
-        P("dp", None),
-        P("dp", None),
-        P(None, None, "dp", "tensor"),
-        P(None, None, "tensor", "dp"),
-        P(None, "tensor", "dp"),
-        P(None, "dp", "tensor"),
-        P(None, "tensor", "dp"),
-        P(None, "tensor", "dp"),
-        P(None, None, ("dp", "tensor")),
-        P(None, None, ("dp", "tensor")),
-    )
-    out_specs = (
-        P("dp", None),
-        P("dp", None),
-        P(None, None, "dp", "tensor"),
-        P(None, None, "tensor", "dp"),
-        P(None, "tensor", "dp"),
-        P(None, "dp", "tensor"),
-        P(None, "tensor", "dp"),
-        P(None, "tensor", "dp"),
-        P(None, None, ("dp", "tensor")),
-        P(None, None, ("dp", "tensor")),
-    )
-    return jax.shard_map(shards, mesh=mesh, in_specs=in_specs, out_specs=out_specs, check_vma=False)
+    n_dp, n_tensor = mesh.shape["dp"], mesh.shape["tensor"]
+    if n_tensor == 4 and n_dp % 2 == 0:
+        sizes = (n_dp // 2, 2, 2, 2)
+        cells = Mesh(mesh.devices.reshape(sizes), CELLS)
+        specs = specs_for(("z", "core"), ("y", "x"))
+        return jax.shard_map(
+            cells_body(sizes), mesh=cells, in_specs=specs, out_specs=specs, check_vma=False
+        )
+    specs = specs_for(("dp",), ("tensor",))
+    return jax.shard_map(shards, mesh=mesh, in_specs=specs, out_specs=specs, check_vma=False)

time: 2290 us -> 867 us (0.38)
  blocking collectives: 685 us -> 25.2 us
  local copies, waits for them, and re-layouts: 553 us -> 78.2 us
  waiting for transfers between devices: 696 us -> 299 us
  Pallas kernels: 0 us -> 87 us
  matrix products: 219 us -> 148 us
  starting transfers between devices: 23.3 us -> 91.2 us
  other arithmetic: 79 us -> 110 us
    unnamed x8 -> x0, blocking collectives: 456 us -> none
    all_gather x16 -> x6, waiting for transfers between devices: 428 us -> 7.75 us  [cells_step(): lax.all_gather(natural(pack), images_axis, axis=0, tiled=True)]
    ppermute x0 -> x71, waiting for transfers between devices: none -> 291 us  [the longest x28 111 us: move(): return lax.ppermute(values, CELLS, moves)]
    unnamed x42 -> x10, waiting for transfers between devices: 268 us -> 0.68 us
    dynamic_update_slice x12 -> x4, local copies, waits for them, and re-layouts: 241 us -> 4.04 us  [cells_step(): lax.dynamic_update_slice(rows, part, (part_start, 0))]
    all_gather x8 -> x2, blocking collectives: 229 us -> 25.2 us  [the longest x1 15.7 us: cells_step(): table = lax.all_gather(small, images_axis, axis=0)]
    unnamed x250 -> x328, local copies, waits for them, and re-layouts: 139 us -> 28 us
    ppermute x0 -> x71, starting transfers between devices: none -> 89.9 us  [the longest x28 41 us: move(): return lax.ppermute(values, CELLS, moves)]
  transfers between devices with their start and end apart: 34 -> 81, of which waited for: 26 -> 28; matrix products, arithmetic and copies ran while one was open for 27% -> 34% of each run, Pallas kernels for 0% -> 10%
where the time goes in v1:
time: 867 us; the launch traced here: 856 us
  waiting for transfers between devices  299 us (34%)
  matrix products  148 us (17%)
  other arithmetic  110 us (13%)
  starting transfers between devices  91.2 us (11%)
  Pallas kernels  87 us (10%)
  local copies, waits for them, and re-layouts  78.2 us (9%)
  blocking collectives  25.2 us (3%)
  between operations  17.4 us (2%)
    dot_general x56, matrix products, product(): lax.dot_general(left, right, dims, preferred_element_type=jnp.float32)  148 us
    ppermute x28, waiting for transfers between devices, move(): return lax.ppermute(values, CELLS, moves)  111 us
    pallas_call x8, Pallas kernels, kernel_call(): pl.pallas_call(kernel, grid=(pairs,), in_specs=[pl.BlockSpec(memory_space...  73.8 us
    ppermute x4, waiting for transfers between devices, gather_quad(): across = lax.ppermute(values, 'x', FLIP)  68.6 us
    ppermute x4, waiting for transfers between devices, reduce_quad(): across = lax.ppermute(across, 'x', FLIP)  60.7 us
    ppermute x28, starting transfers between devices, move(): return lax.ppermute(values, CELLS, moves)  41 us
    ppermute x26, starting transfers between devices, flip(): return lax.ppermute(values, 'core', FLIP)  33.4 us
    ppermute x3, waiting for transfers between devices, total_of(): come = lax.ppermute(table, axis, FLIP)  31 us
  transfers between devices with their start and end apart: 81, of which 28 were waited for; matrix products, arithmetic and copies ran while one was open for 34% of the time, Pallas kernels for 10%

profile of v1, /device:TPU:0, one launch (start us, length us, event | category | flops | bytes accessed | tf_op | source)
XLA Modules:
  0.0 856.4 jit_solution(8208871799119658210)
XLA Ops:
  12.7 15.7 %all-gather = f32[192,32]{1,0:T(8,128)S(1)} all-gather(f32[24,32]{1,0:T(8,128)S(1)} %pad_maximum_fusion.26), channel_id=2, replica_groups=mesh['z'=4,'core'=2,'y'=2,'x'=2] {'z','core'}, dimensions={0}, use_global_device_ids=true | all-gather | bytes 27648 | tf_op jit(solution)/shard_map/all_gather | solution.py:878
  28.4 9.5 %all-gather.1 = f32[32,24,32]{2,1,0:T(8,128)S(1)} all-gather(f32[8,24,32]{2,1,0:T(8,128)S(1)} %bitcast.251), channel_id=3, replica_groups=mesh['z'=4,'core'=2,'y'=2,'x'=2] {'y','x'}, dimensions={0}, use_global_device_ids=true | all-gather | bytes 122880 | tf_op jit(solution)/shard_map/all_gather | solution.py:879
  82.9 15.2 %collective-permute-done.3 = bf16[1024,1024]{1,0:T(8,128)(2,1)} collective-permute-done((bf16[1024,1024]{1,0:T(8,128)(2,1)}, bf16[1024,1024]{1,0:T(8,128)(2,1)}, u32[]{:S(2)}, u32[]{:S(2)}) %collective-permute-start.3) | collective-permute-done | bytes 2097184 | tf_op jit(solution)/shard_map/ppermute | solution.py:691
  126.7 8.1 shard_map.177
  161.8 19.9 %collective-permute-done.9 = bf16[448,1024]{1,0:T(8,128)(2,1)} collective-permute-done((bf16[448,1024]{1,0:T(8,128)(2,1)S(1)}, bf16[448,1024]{1,0:T(8,128)(2,1)}, u32[]{:S(2)}, u32[]{:S(2)}) %collective-permute-start.9) | collective-permute-done | bytes 917536 | tf_op jit(solution)/shard_map/ppermute | solution.py:748
  196.0 34.1 %collective-permute-done.12 = bf16[1024,1024]{1,0:T(8,128)(2,1)} collective-permute-done((bf16[1024,1024]{1,0:T(8,128)(2,1)}, bf16[1024,1024]{1,0:T(8,128)(2,1)}, u32[]{:S(2)}, u32[]{:S(2)}) %collective-permute-start.12) | collective-permute-done | bytes 2097184 | tf_op jit(solution)/shard_map/ppermute | solution.py:691
  244.1 14.4 %collective-permute-done.15 = bf16[448,1024]{1,0:T(8,128)(2,1)S(1)} collective-permute-done((bf16[448,1024]{1,0:T(8,128)(2,1)S(1)}, bf16[448,1024]{1,0:T(8,128)(2,1)S(1)}, u32[]{:S(2)}, u32[]{:S(2)}) %collective-permute-start.15) | collective-permute-done | bytes 917536 | tf_op jit(solution)/shard_map/ppermute | solution.py:758
  279.7 8.1 shard_map.179
  291.4 6.4 shard_map.180
  324.7 14.6 %collective-permute-done.26 = bf16[448,1024]{1,0:T(8,128)(2,1)} collective-permute-done((bf16[448,1024]{1,0:T(8,128)(2,1)S(1)}, bf16[448,1024]{1,0:T(8,128)(2,1)}, u32[]{:S(2)}, u32[]{:S(2)}) %collective-permute-start.26) | collective-permute-done | bytes 917536 | tf_op jit(solution)/shard_map/ppermute | solution.py:748
  343.5 14.4 %collective-permute-done.23 = bf16[448,1024]{1,0:T(8,128)(2,1)} collective-permute-done((bf16[448,1024]{1,0:T(8,128)(2,1)}, bf16[448,1024]{1,0:T(8,128)(2,1)}, u32[]{:S(2)}, u32[]{:S(2)}) %collective-permute-start.23) | collective-permute-done | bytes 917536 | tf_op jit(solution)/shard_map/ppermute | solution.py:748
  362.3 6.9 multiply_convert_fusion
  369.5 13.6 %fusion.10 = (f32[1024]{0:T(1024)}, bf16[1792,1024]{1,0:T(8,128)(2,1)S(1)}, f32[1792,1024]{1,0:T(8,128)S(1)}) fusion(f32[1792,1024]{1,0:T(8,128)} %get-tuple-element.357, f32[1024]{0:T(1024)S(1)} %add.574, bf16[1024,1024]{1,0:T(8,128)(2,1)S(1)} %broadcast_select_fusion, bf16[448,1024]{1,0:T(8,128)(2,1)S(1)} %collective-permute-done.24, ...), kind=kOutput, calls=%fused_computation.17 | convolution fusion | flops 3796630528 | bytes 24125440 | tf_op jit(solution)/shard_map/dot_general | solution.py:398
  394.1 6.9 convolution_convert_fusion.2
  402.3 14.2 %collective-permute-done.32 = bf16[448,1024]{1,0:T(8,128)(2,1)S(1)} collective-permute-done((bf16[448,1024]{1,0:T(8,128)(2,1)S(1)}, bf16[448,1024]{1,0:T(8,128)(2,1)S(1)}, u32[]{:S(2)}, u32[]{:S(2)}) %collective-permute-start.32) | collective-permute-done | bytes 917536 | tf_op jit(solution)/shard_map/ppermute | solution.py:758
  433.6 19.3 %collective-permute-done.35 = bf16[448,1024]{1,0:T(8,128)(2,1)S(1)} collective-permute-done((bf16[448,1024]{1,0:T(8,128)(2,1)S(1)}, bf16[448,1024]{1,0:T(8,128)(2,1)S(1)}, u32[]{:S(2)}, u32[]{:S(2)}) %collective-permute-start.35) | collective-permute-done | bytes 917536 | tf_op jit(solution)/shard_map/ppermute | solution.py:758
  463.7 9.3 %shard_map.181 = (f32[304,768]{1,0:T(8,128)}, f32[304,768]{1,0:T(8,128)}, bf16[304,512]{1,0:T(8,128)(2,1)}, bf16[304,512]{1,0:T(8,128)(2,1)}, f32[2,8,128]{2,1,0:T(8,128)}) custom-call(s32[4]{0:T(128)} %pad_add_fusion.place, bf16[896,768]{1,0:T(8,128)(2,1)} %copy-done.9, bf16[896,768]{1,0:T(8,128)(2,1)} %copy-done.10, ...), custom_call_target="tpu_custom_call" | custom-call | tf_op jit(solution)/shard_map/pallas_call | solution.py:545
  474.5 13.2 %shard_map.182 = (bf16[896,768]{1,0:T(8,128)(2,1)}, bf16[896,768]{1,0:T(8,128)(2,1)}, f32[2,8,128]{2,1,0:T(8,128)}) custom-call(s32[4]{0:T(128)} %pad_add_fusion.place, bf16[896,768]{1,0:T(8,128)(2,1)} %copy-done.9, bf16[896,768]{1,0:T(8,128)(2,1)} %copy-done.10, bf16[896,256]{1,0:T(8,128)(2,1)} %convolution_convert_fusion.23.up_a, ...), custom_call_target="tpu_custom_call" | custom-call | tf_op jit(solution)/shard_map/pallas_call | solution.py:545
  512.5 19.7 %collective-permute-done.46 = bf16[448,1024]{1,0:T(8,128)(2,1)} collective-permute-done((bf16[448,1024]{1,0:T(8,128)(2,1)S(1)}, bf16[448,1024]{1,0:T(8,128)(2,1)}, u32[]{:S(2)}, u32[]{:S(2)}) %collective-permute-start.46) | collective-permute-done | bytes 917536 | tf_op jit(solution)/shard_map/ppermute | solution.py:748
  532.2 7.1 fusion.9
  542.7 6.5 fusion.12
  568.7 12.8 %collective-permute-done.50 = bf16[448,1024]{1,0:T(8,128)(2,1)S(1)} collective-permute-done((bf16[448,1024]{1,0:T(8,128)(2,1)S(1)}, bf16[448,1024]{1,0:T(8,128)(2,1)S(1)}, u32[]{:S(2)}, u32[]{:S(2)}) %collective-permute-start.50) | collective-permute-done | bytes 917536 | tf_op jit(solution)/shard_map/ppermute | solution.py:758
  584.8 9.6 %collective-permute-start.53 = (bf16[448,1024]{1,0:T(8,128)(2,1)S(1)}, bf16[448,1024]{1,0:T(8,128)(2,1)S(1)}, u32[]{:S(2)}, u32[]{:S(2)}) collective-permute-start(bf16[448,1024]{1,0:T(8,128)(2,1)S(1)} %convert_element_type.381), channel_id=1, source_target_pairs={{0,4},{4,0},{1,5},{5,1},{2,6},{6,2},{3,7},{7,3},{8,12},{12,8},{9,1... | collective-permute-start | bytes 2752520 | tf_op jit(solution)/shard_map/ppermute | solution.py:778
  608.5 9.3 %shard_map.183 = (f32[304,768]{1,0:T(8,128)}, f32[304,768]{1,0:T(8,128)}, bf16[304,512]{1,0:T(8,128)(2,1)}, bf16[304,512]{1,0:T(8,128)(2,1)}, f32[2,8,128]{2,1,0:T(8,128)}) custom-call(s32[4]{0:T(128)} %pad_add_fusion.place, bf16[896,768]{1,0:T(8,128)(2,1)} %copy-done.7, bf16[896,768]{1,0:T(8,128)(2,1)} %copy-done.8, ...), custom_call_target="tpu_custom_call" | custom-call | tf_op jit(solution)/shard_map/pallas_call | solution.py:545
  619.3 8.3 convolution_convert_fusion
  627.7 13.0 %shard_map.184 = (bf16[896,768]{1,0:T(8,128)(2,1)}, bf16[896,768]{1,0:T(8,128)(2,1)}, f32[2,8,128]{2,1,0:T(8,128)}) custom-call(s32[4]{0:T(128)} %pad_add_fusion.place, bf16[896,768]{1,0:T(8,128)(2,1)} %copy-done.7, bf16[896,768]{1,0:T(8,128)(2,1)} %copy-done.8, bf16[896,256]{1,0:T(8,128)(2,1)} %convolution_convert_fusion.21.up_a, ...), custom_call_target="tpu_custom_call" | custom-call | tf_op jit(solution)/shard_map/pallas_call | solution.py:545
  699.1 25.2 %collective-permute-done.65 = f32[24,1024]{1,0:T(8,128)S(1)} collective-permute-done((f32[24,1024]{1,0:T(8,128)S(1)}, f32[24,1024]{1,0:T(8,128)S(1)}, u32[]{:S(2)}, u32[]{:S(2)}) %collective-permute-start.65) | collective-permute-done | bytes 98336 | tf_op jit(solution)/shard_map/ppermute | solution.py:766
  754.0 15.8 %collective-permute-done.39.round_11 = bf16[448,1024]{1,0:T(8,128)(2,1)S(1)} collective-permute-done((bf16[448,1024]{1,0:T(8,128)(2,1)S(1)}, bf16[448,1024]{1,0:T(8,128)(2,1)S(1)}, u32[]{:S(2)}, u32[]{:S(2)}) %collective-permute-start.39) | collective-permute-done | bytes 917536 | tf_op jit(solution)/shard_map/ppermute | solution.py:691
  770.7 19.0 %collective-permute-done.38.round_10 = bf16[448,1024]{1,0:T(8,128)(2,1)S(1)} collective-permute-done((bf16[448,1024]{1,0:T(8,128)(2,1)S(1)}, bf16[448,1024]{1,0:T(8,128)(2,1)S(1)}, u32[]{:S(2)}, u32[]{:S(2)}) %collective-permute-start.38) | collective-permute-done | bytes 917536 | tf_op jit(solution)/shard_map/ppermute | solution.py:691
  795.6 6.7 give_rows.2
  809.4 20.3 %collective-permute-done.62.round_01 = bf16[448,1024]{1,0:T(8,128)(2,1)} collective-permute-done((bf16[448,1024]{1,0:T(8,128)(2,1)S(1)}, bf16[448,1024]{1,0:T(8,128)(2,1)}, u32[]{:S(2)}, u32[]{:S(2)}) %collective-permute-start.62) | collective-permute-done | bytes 917536 | tf_op jit(solution)/shard_map/ppermute | solution.py:691
  829.7 6.5 give_rows.3
  (761 shorter events, 415.4 us)
Async XLA Ops:
  7.2 36.5 %all-gather.9.cloned.1.call-start = ((), (), s32[]{:S(2)}) async-start(), calls=%async_computation.4 | async-start | bytes 2359296 | tf_op jit(solution)/shard_map/all_gather | solution.py:859
  11.5 149.3 %all-gather.11.cloned.1.call-start = ((), (), s32[]{:S(2)}) async-start(), calls=%async_computation.5 | async-start | bytes 2359296 | tf_op jit(solution)/shard_map/all_gather | solution.py:859
  12.4 169.3 %all-gather.13.cloned.1.call-start = ((), (), s32[]{:S(2)}) async-start(), calls=%async_computation.6 | async-start | bytes 2359296 | tf_op jit(solution)/shard_map/all_gather | solution.py:859
  67.3 117.0 %all-gather.15.cloned.1.call-start = ((), (), s32[]{:S(2)}) async-start(), calls=%async_computation.7 | async-start | bytes 2359296 | tf_op jit(solution)/shard_map/all_gather | solution.py:859
  154.3 161.7 %all-gather.19.cloned.1.call-start = ((), (), s32[]{:S(2)}) async-start(), calls=%async_computation.9 | async-start | bytes 2359296 | tf_op jit(solution)/shard_map/all_gather | solution.py:859
  160.7 27.1 %collective-permute-start.11 = (bf16[1024,1024]{1,0:T(8,128)(2,1)}, bf16[1024,1024]{1,0:T(8,128)(2,1)}, u32[]{:S(2)}, u32[]{:S(2)}) collective-permute-start(bf16[1024,1024]{1,0:T(8,128)(2,1)} %all-gather.11.cloned.1.call-done), channel_id=1, source_target_pairs={{0,2},{1,3},{2,6},{3,7},{4,0},{5,1},{6,4},{7,5},{8,10},{9,11},{10,... | collective-permute-start | bytes 6291464 | tf_op jit(solution)/shard_map/ppermute | solution.py:691
  181.6 48.5 %collective-permute-start.12 = (bf16[1024,1024]{1,0:T(8,128)(2,1)}, bf16[1024,1024]{1,0:T(8,128)(2,1)}, u32[]{:S(2)}, u32[]{:S(2)}) collective-permute-start(bf16[1024,1024]{1,0:T(8,128)(2,1)} %all-gather.13.cloned.1.call-done), channel_id=1, source_target_pairs={{0,2},{1,3},{2,6},{3,7},{4,0},{5,1},{6,4},{7,5},{8,10},{9,11},{10,... | collective-permute-start | bytes 6291464 | tf_op jit(solution)/shard_map/ppermute | solution.py:691
  184.3 51.0 %collective-permute-start.17 = (bf16[1024,1024]{1,0:T(8,128)(2,1)}, bf16[1024,1024]{1,0:T(8,128)(2,1)S(1)}, u32[]{:S(2)}, u32[]{:S(2)}) collective-permute-start(bf16[1024,1024]{1,0:T(8,128)(2,1)} %all-gather.15.cloned.1.call-done), channel_id=1, source_target_pairs={{0,1},{1,0},{2,3},{3,2},{4,6},{5,7},{6,4},{7,5},{8,9},{9,8},{10,11... | collective-permute-start | bytes 6291464 | tf_op jit(solution)/shard_map/ppermute | solution.py:691
  260.8 80.4 %all-gather.17.cloned.1.call-start = ((), (), s32[]{:S(2)}) async-start(), calls=%async_computation.8 | async-start | bytes 2359296 | tf_op jit(solution)/shard_map/all_gather | solution.py:859
  310.8 338.9 %reduce-scatter.5.cloned.1.call-start = ((), (), s32[]{:S(2)}) async-start(), calls=%async_computation.10 | async-start | bytes 4718592 | tf_op jit(solution)/shard_map/reduce_scatter | solution.py:726
  316.0 44.5 %collective-permute-start.28 = (bf16[1024,1024]{1,0:T(8,128)(2,1)}, bf16[1024,1024]{1,0:T(8,128)(2,1)}, u32[]{:S(2)}, u32[]{:S(2)}) collective-permute-start(bf16[1024,1024]{1,0:T(8,128)(2,1)} %all-gather.19.cloned.1.call-done), channel_id=1, source_target_pairs={{0,2},{1,3},{2,6},{3,7},{4,0},{5,1},{6,4},{7,5},{8,10},{9,11},{10,... | collective-permute-start | bytes 6291464 | tf_op jit(solution)/shard_map/ppermute | solution.py:691
  322.7 35.3 %collective-permute-start.23 = (bf16[448,1024]{1,0:T(8,128)(2,1)}, bf16[448,1024]{1,0:T(8,128)(2,1)}, u32[]{:S(2)}, u32[]{:S(2)}) collective-permute-start(bf16[448,1024]{1,0:T(8,128)(2,1)} %convert_element_type.335), channel_id=1, source_target_pairs={{0,1},{1,0},{2,3},{3,2},{4,5},{5,4},{6,7},{7,6},{8,9},{9,8},{10,11... | collective-permute-start | bytes 2752520 | tf_op jit(solution)/shard_map/ppermute | solution.py:748
  324.7 33.3 %collective-permute-start.25 = (bf16[448,1024]{1,0:T(8,128)(2,1)S(1)}, bf16[448,1024]{1,0:T(8,128)(2,1)}, u32[]{:S(2)}, u32[]{:S(2)}) collective-permute-start(bf16[448,1024]{1,0:T(8,128)(2,1)S(1)} %add_convert_fusion.10), channel_id=1, source_target_pairs={{0,4},{4,0},{1,5},{5,1},{2,6},{6,2},{3,7},{7,3},{8,12},{12,8},{9,1... | collective-permute-start | bytes 2752520 | tf_op jit(solution)/shard_map/ppermute | solution.py:778
  341.2 28.0 %collective-permute-start.29 = (bf16[1024,1024]{1,0:T(8,128)(2,1)}, bf16[1024,1024]{1,0:T(8,128)(2,1)}, u32[]{:S(2)}, u32[]{:S(2)}) collective-permute-start(bf16[1024,1024]{1,0:T(8,128)(2,1)} %all-gather.17.cloned.1.call-done), channel_id=1, source_target_pairs={{0,2},{1,3},{2,6},{3,7},{4,0},{5,1},{6,4},{7,5},{8,10},{9,11},{10,... | collective-permute-start | bytes 6291464 | tf_op jit(solution)/shard_map/ppermute | solution.py:691
  401.0 86.7 %collective-permute-start.42 = (bf16[1024,1024]{1,0:T(8,128)(2,1)}, bf16[1024,1024]{1,0:T(8,128)(2,1)}, u32[]{:S(2)}, u32[]{:S(2)}) collective-permute-start(bf16[1024,1024]{1,0:T(8,128)(2,1)} %convolution_convert_fusion.2), channel_id=1, source_target_pairs={{0,4},{1,5},{2,0},{3,1},{4,6},{5,7},{6,2},{7,3},{8,12},{9,13},{10,... | collective-permute-start | bytes 6291464 | tf_op jit(solution)/shard_map/ppermute | solution.py:691
  424.4 63.3 %collective-permute-start.41 = (bf16[1024,1024]{1,0:T(8,128)(2,1)}, bf16[1024,1024]{1,0:T(8,128)(2,1)S(1)}, u32[]{:S(2)}, u32[]{:S(2)}) collective-permute-start(bf16[1024,1024]{1,0:T(8,128)(2,1)} %convolution_convert_fusion.3), channel_id=1, source_target_pairs={{0,4},{1,5},{2,0},{3,1},{4,6},{5,7},{6,2},{7,3},{8,12},{9,13},{10,... | collective-permute-start | bytes 6291464 | tf_op jit(solution)/shard_map/ppermute | solution.py:691
  512.5 29.6 %collective-permute-start.45 = (bf16[448,1024]{1,0:T(8,128)(2,1)S(1)}, bf16[448,1024]{1,0:T(8,128)(2,1)}, u32[]{:S(2)}, u32[]{:S(2)}) collective-permute-start(bf16[448,1024]{1,0:T(8,128)(2,1)S(1)} %convert_element_type.369), channel_id=1, source_target_pairs={{0,4},{4,0},{1,5},{5,1},{2,6},{6,2},{3,7},{7,3},{8,12},{12,8},{9,1... | collective-permute-start | bytes 2752520 | tf_op jit(solution)/shard_map/ppermute | solution.py:778
  539.3 296.9 %reduce-scatter.9.cloned.1.call-start = ((), (), s32[]{:S(2)}) async-start(), calls=%async_computation.12 | async-start | bytes 2359296 | tf_op jit(solution)/shard_map/reduce_scatter | solution.py:726
  599.8 81.2 %collective-permute-start.57 = (bf16[1024,1024]{1,0:T(8,128)(2,1)}, bf16[1024,1024]{1,0:T(8,128)(2,1)}, u32[]{:S(2)}, u32[]{:S(2)}) collective-permute-start(bf16[1024,1024]{1,0:T(8,128)(2,1)} %convolution_convert_fusion.1), channel_id=1, source_target_pairs={{0,4},{1,5},{2,0},{3,1},{4,6},{5,7},{6,2},{7,3},{8,12},{9,13},{10,... | collective-permute-start | bytes 6291464 | tf_op jit(solution)/shard_map/ppermute | solution.py:691
  601.9 44.0 %collective-permute-start.54 = (bf16[1024,1024]{1,0:T(8,128)(2,1)}, bf16[1024,1024]{1,0:T(8,128)(2,1)}, u32[]{:S(2)}, u32[]{:S(2)}) collective-permute-start(bf16[1024,1024]{1,0:T(8,128)(2,1)} %fusion.32), channel_id=1, source_target_pairs={{0,1},{1,0},{2,3},{3,2},{4,6},{5,7},{6,4},{7,5},{8,9},{9,8},{10,11... | collective-permute-start | bytes 6291464 | tf_op jit(solution)/shard_map/ppermute | solution.py:691
  627.6 53.5 %collective-permute-start.58 = (bf16[1024,1024]{1,0:T(8,128)(2,1)}, bf16[1024,1024]{1,0:T(8,128)(2,1)}, u32[]{:S(2)}, u32[]{:S(2)}) collective-permute-start(bf16[1024,1024]{1,0:T(8,128)(2,1)} %convolution_convert_fusion), channel_id=1, source_target_pairs={{0,4},{1,5},{2,0},{3,1},{4,6},{5,7},{6,2},{7,3},{8,12},{9,13},{10,... | collective-permute-start | bytes 6291464 | tf_op jit(solution)/shard_map/ppermute | solution.py:691
  649.6 191.7 %reduce-scatter.7.cloned.1.call-start = ((), (), s32[]{:S(2)}) async-start(), calls=%async_computation.11 | async-start | bytes 2359296 | tf_op jit(solution)/shard_map/reduce_scatter | solution.py:726
  666.4 27.3 %collective-permute-start.60 = (bf16[512,1024]{1,0:T(8,128)(2,1)}, bf16[512,1024]{1,0:T(8,128)(2,1)}, u32[]{:S(2)}, u32[]{:S(2)}) collective-permute-start(bf16[512,1024]{1,0:T(8,128)(2,1)} %get-tuple-element.273), channel_id=1, source_target_pairs={{4,5},{5,4},{6,7},{7,6},{12,13},{13,12},{14,15},{15,14},{20,21},{2... | collective-permute-start | bytes 3145736 | tf_op jit(solution)/shard_map/ppermute | solution.py:691
  696.4 46.0 %collective-permute-start.70 = (bf16[1024,1024]{1,0:T(8,128)(2,1)}, bf16[1024,1024]{1,0:T(8,128)(2,1)}, u32[]{:S(2)}, u32[]{:S(2)}) collective-permute-start(bf16[1024,1024]{1,0:T(8,128)(2,1)} %fusion.33), channel_id=1, source_target_pairs={{0,1},{1,0},{2,3},{3,2},{4,6},{5,7},{6,4},{7,5},{8,9},{9,8},{10,11... | collective-permute-start | bytes 6291464 | tf_op jit(solution)/shard_map/ppermute | solution.py:691
  746.1 99.5 %reduce-scatter.11.cloned.1.call-start = ((), (), s32[]{:S(2)}) async-start(), calls=%async_computation.13 | async-start | bytes 4718592 | tf_op jit(solution)/shard_map/reduce_scatter | solution.py:726
  747.5 42.1 %collective-permute-start.38 = (bf16[448,1024]{1,0:T(8,128)(2,1)S(1)}, bf16[448,1024]{1,0:T(8,128)(2,1)S(1)}, u32[]{:S(2)}, u32[]{:S(2)}) collective-permute-start(bf16[448,1024]{1,0:T(8,128)(2,1)S(1)} %copy-done.31), channel_id=1, source_target_pairs={{0,1},{1,0},{2,5},{3,4},{4,3},{5,2},{6,7},{7,6},{8,9},{9,8},{10,13... | collective-permute-start | bytes 2752520 | tf_op jit(solution)/shard_map/ppermute | solution.py:691
  748.8 42.1 %collective-permute-start.36 = (bf16[448,1024]{1,0:T(8,128)(2,1)S(1)}, bf16[448,1024]{1,0:T(8,128)(2,1)S(1)}, u32[]{:S(2)}, u32[]{:S(2)}) collective-permute-start(bf16[448,1024]{1,0:T(8,128)(2,1)S(1)} %copy-done.31), channel_id=1, source_target_pairs={{2,4},{3,5},{4,2},{5,3},{10,12},{11,13},{12,10},{13,11},{18,20},{1... | collective-permute-start | bytes 2752520 | tf_op jit(solution)/shard_map/ppermute | solution.py:691
  749.5 46.1 %collective-permute-start.37 = (bf16[448,1024]{1,0:T(8,128)(2,1)S(1)}, bf16[448,1024]{1,0:T(8,128)(2,1)}, u32[]{:S(2)}, u32[]{:S(2)}) collective-permute-start(bf16[448,1024]{1,0:T(8,128)(2,1)S(1)} %copy-done.31), channel_id=1, source_target_pairs={{0,2},{1,3},{2,6},{3,7},{4,0},{5,1},{6,4},{7,5},{8,10},{9,11},{10,... | collective-permute-start | bytes 2752520 | tf_op jit(solution)/shard_map/ppermute | solution.py:691
  752.4 50.1 %collective-permute-start.61 = (bf16[448,1024]{1,0:T(8,128)(2,1)S(1)}, bf16[448,1024]{1,0:T(8,128)(2,1)}, u32[]{:S(2)}, u32[]{:S(2)}) collective-permute-start(bf16[448,1024]{1,0:T(8,128)(2,1)S(1)} %copy-done.36), channel_id=1, source_target_pairs={{2,4},{3,5},{4,2},{5,3},{10,12},{11,13},{12,10},{13,11},{18,20},{1... | collective-permute-start | bytes 2752520 | tf_op jit(solution)/shard_map/ppermute | solution.py:691
  769.8 39.6 %collective-permute-start.63 = (bf16[448,1024]{1,0:T(8,128)(2,1)S(1)}, bf16[448,1024]{1,0:T(8,128)(2,1)}, u32[]{:S(2)}, u32[]{:S(2)}) collective-permute-start(bf16[448,1024]{1,0:T(8,128)(2,1)S(1)} %copy-done.36), channel_id=1, source_target_pairs={{0,1},{1,0},{2,5},{3,4},{4,3},{5,2},{6,7},{7,6},{8,9},{9,8},{10,13... | collective-permute-start | bytes 2752520 | tf_op jit(solution)/shard_map/ppermute | solution.py:691
  789.6 40.1 %collective-permute-start.62 = (bf16[448,1024]{1,0:T(8,128)(2,1)S(1)}, bf16[448,1024]{1,0:T(8,128)(2,1)}, u32[]{:S(2)}, u32[]{:S(2)}) collective-permute-start(bf16[448,1024]{1,0:T(8,128)(2,1)S(1)} %copy-done.36), channel_id=1, source_target_pairs={{0,2},{1,3},{2,6},{3,7},{4,0},{5,1},{6,4},{7,5},{8,10},{9,11},{10,... | collective-permute-start | bytes 2752520 | tf_op jit(solution)/shard_map/ppermute | solution.py:691
  790.9 38.8 %collective-permute-start.64 = (bf16[448,1024]{1,0:T(8,128)(2,1)S(1)}, bf16[448,1024]{1,0:T(8,128)(2,1)}, u32[]{:S(2)}, u32[]{:S(2)}) collective-permute-start(bf16[448,1024]{1,0:T(8,128)(2,1)S(1)} %copy-done.36), channel_id=1, source_target_pairs={{0,3},{1,2},{2,7},{3,6},{4,1},{5,0},{6,5},{7,4},{8,11},{9,10},{10,... | collective-permute-start | bytes 2752520 | tf_op jit(solution)/shard_map/ppermute | solution.py:691
  (197 other events, 1931.4 us)
Sparse Core Ops, SparseCore 0:
  11.6 32.1 all-gather.8
  45.4 28.4 all-gather.10
  75.5 28.5 all-gather.12
  154.4 27.9 all-gather.14
  260.9 30.3 all-gather.18
  310.9 30.2 all-gather.16
  539.5 49.2 reduce-scatter.4
  649.7 38.9 reduce-scatter.8
  746.2 33.6 reduce-scatter.6
  782.0 48.6 reduce-scatter.10

commit v2 on v1

--- a/solution.py
+++ b/solution.py
@@ -1,3 +1,6 @@
+import dataclasses
+from typing import Any
+
 import jax
 import jax.numpy as jnp
 import numpy as np
@@ -365,12 +368,24 @@
     )
 
 
+ATT, MLP = range(2)
+
+
+@dataclasses.dataclass
+class Stream:
+    grads: Any
+    pack: int
+    held: Any
+    step: int
+    home: Any
+
+
 CELLS = ("z", "core", "y", "x")
 PHASES = {
-    (1, 4): (("mlp", 1),),
-    (0, 1): (("att", 1),),
-    (0, 4): (("att", 1), ("mlp", 1)),
-    (0, 5): (("mlp", 0),),
+    (1, 4): ((MLP, 1),),
+    (0, 1): ((ATT, 1),),
+    (0, 4): ((ATT, 1), (MLP, 1)),
+    (0, 5): ((MLP, 0),),
 }
 FLIP = ((0, 1), (1, 0))
 TILE = 16
@@ -543,14 +558,14 @@
 
 def kernel_call(kernel, pairs, ins, in_specs, outs, out_specs):
     return pl.pallas_call(
-        kernel,
-        grid=(pairs,),
-        in_specs=[pl.BlockSpec(memory_space=pltpu.SMEM)] + in_specs,
-        out_specs=out_specs,
-        out_shape=[jax.ShapeDtypeStruct(shape, kind) for shape, kind in outs],
-        compiler_params=pltpu.CompilerParams(
-            dimension_semantics=("arbitrary",), vmem_limit_bytes=VMEM_LIMIT
-        ),
+kernel,
+grid=(pairs,),
+in_specs=[pl.BlockSpec(memory_space=pltpu.SMEM)] + in_specs,
+out_specs=out_specs,
+out_shape=[jax.ShapeDtypeStruct(shape, kind) for shape, kind in outs],
+compiler_params=pltpu.CompilerParams(
+    dimension_semantics=("arbitrary",), vmem_limit_bytes=VMEM_LIMIT
+),
     )(*ins)
 
 
@@ -644,7 +659,6 @@
         grid_spec=grid_spec,
         out_shape=jax.ShapeDtypeStruct((3 * SEQ, width), jnp.float32),
         compiler_params=pltpu.CompilerParams(vmem_limit_bytes=VMEM_LIMIT),
-        name="give_rows",
     )(place, *rounds)
 
 
@@ -670,6 +684,9 @@
     n_z, _, _, _ = sizes
     trade = cell_moves(
         sizes, lambda z, c, y, x: (z, c, y, 1 - x) if c == 0 else (z, c, 1 - y, x)
+    )
+    cross = cell_moves(
+        sizes, lambda z, c, y, x: (z, c, y, 1 - x) if c == 1 else (z, c, 1 - y, x)
     )
     relay_y = cell_moves(
         sizes, lambda z, c, y, x: (z, 1, 1 - y, x) if c == 0 else (z, 0, y, x)
@@ -726,22 +743,21 @@
         return lax.psum_scatter(mine, images_axis, scatter_dimension=0, tiled=True)
 
     def start_stream(grads, pack):
-        return {"grads": grads, "pack": pack, "held": collect_far(grads[1]), "step": 0}
+        return Stream(grads, pack, collect_far(grads[1]), 0, None)
 
     def start_pair(grads, home, pack):
         held = [move(grad, repay) for grad in grads]
-        return {"grads": (None, grads), "pack": pack, "held": held, "step": 1, "home": home}
+        return Stream((None, grads), pack, held, 1, home)
 
     def advance(value, stream, core):
-        value, held = tie(value, stream["held"])
-        step = stream["step"]
-        if step == 0:
-            held = collect_near(stream["grads"][0], held, core)
-        elif step == 1:
-            home = stream.get("home", core == 0)
-            value, held = tie(value, collect_end(stream["grads"][1], held, home))
+        value, held = tie(value, stream.held)
+        if stream.step == 0:
+            held = collect_near(stream.grads[0], held, core)
+        elif stream.step == 1:
+            home = core == 0 if stream.home is None else stream.home
+            value, held = tie(value, collect_end(stream.grads[1], held, home))
             held = collect_sum(held)
-        stream["held"], stream["step"] = held, step + 1
+        stream.held, stream.step = held, stream.step + 1
         return value
 
     def gather_quad(values):
@@ -762,15 +778,17 @@
         return own + near.astype(jnp.float32) + across.astype(jnp.float32)
 
     def total_of(table):
-        for axis in ("x", "y", "core"):
-            come = lax.ppermute(table, axis, FLIP)
-            table = table + come
+        come = flip(table)
+        table = table + come
+        table = table + move(table, cross)
+        table = flip(table)
+        table = table + move(table, cross)
         gap = 1
         while gap < n_z:
             if n_z % (2 * gap):
-                return lax.psum(table, "z")
+                return lax.psum(table, CELLS[0])
             partner = [(z, z ^ gap) for z in range(n_z)]
-            table = table + lax.ppermute(table, "z", partner)
+            table = table + lax.ppermute(table, CELLS[0], partner)
             gap *= 2
         return table
 
@@ -877,11 +895,8 @@
         n_gain, n_bias, n_qv = 2 * LAYERS, 4 * LAYERS, b_qv.size // piece
         table = lax.all_gather(small, images_axis, axis=0)
         table = lax.all_gather(table, chips, axis=0)
-        inputs, grad_out, table, _ = tie(inputs, grad_out, table, whole[0])
+        inputs, table, _ = tie(inputs, table, whole[0])
         stream = take_share(inputs, core, y, x)
-        cotangent = take_share(grad_out, core, y, x)
-        stream, cotangent = tie(stream, cotangent)
-        first_rows = gather_quad(cotangent.astype(jnp.bfloat16))
         tokens = jnp.transpose(table[:, :, : n_gain + n_bias], (2, 1, 0, 3)).reshape(-1, width)
         gains = tokens[:n_gain].reshape(LAYERS, 2, width)
         shifts = tokens[n_gain:].reshape(LAYERS, 4, width)
@@ -952,6 +967,11 @@
                 middle, gains[layer, 1], shifts[layer, 2]
             )
             rows_two = gather_quad(normed_two.astype(jnp.bfloat16))
+            if layer == 0:
+                cotangent, normed_two = tie(grad_out, normed_two)
+                cotangent = take_share(cotangent, core, y, x)
+                rows_two, cotangent = tie(rows_two, cotangent)
+                first_rows = gather_quad(cotangent.astype(jnp.bfloat16))
             rows_two = lent(3 * layer + 1, rows_two)
             up_w = weights[3 * layer + 1]
             hidden = product(rows_two, up_w, NN) + up_bias[layer]
@@ -1020,7 +1040,7 @@
             back_two = reduce_quad(hidden_rows, up_w, NT)
             grad_down = natural(product(cot_rows, activation, TN).astype(jnp.bfloat16))
             grad_up = natural(product(rows_two, hidden_rows, TN).astype(jnp.bfloat16))
-            streams["mlp", layer] = start_pair([grad_up, grad_down], home, 3 * layer + 1)
+            streams[MLP, layer] = start_pair([grad_up, grad_down], home, 3 * layer + 1)
             back_two = advance_all(back_two, layer, 1)
             if layer == LAYERS - 1:
                 back_two, last = tie(back_two, activation)
@@ -1062,7 +1082,7 @@
                 natural(jnp.concatenate([grad_att[slot], grad_out_w[slot]], axis=1))
                 for slot in range(2)
             ]
-            streams["att", layer] = start_stream(grad_att, 3 * layer)
+            streams[ATT, layer] = start_stream(grad_att, 3 * layer)
             qkv_w = [slot[:, : 3 * local] for slot in att_w]
             back_one = reduce_pair(grad_qkv, qkv_w, NT)
             back_one = advance_all(back_one, layer, 5)
@@ -1074,7 +1094,7 @@
                 [gain_one, gain_two],
                 [shift_one, shift_out, shift_two, shift_down],
             )
-        cotangent = advance(cotangent, streams["att", 0], core)
+        cotangent = advance(cotangent, streams[ATT, 0], core)
         every_back = share_rows(cotangent, home)
         rows = [row for layer in range(LAYERS) for row in token_grads[layer][0]]
         rows += [row for layer in range(LAYERS) for row in token_grads[layer][1]]
@@ -1091,11 +1111,11 @@
             spot = lax.broadcasted_iota(jnp.int32, (4, 1), 0) == up_quarter
             table.append(jnp.where(spot, unit_grads[layer][None], 0.0))
         table = total_of(jnp.concatenate(table, axis=0))
-        table = advance(table, streams["att", 0], core)
+        table = advance(table, streams[ATT, 0], core)
+        full_out = give_call(place, every_out)
         for stream in streams.values():
-            while stream["step"] < 3:
+            while stream.step < 3:
                 advance((), stream, core)
-        full_out = give_call(place, every_out)
         full_back = give_call(place, every_back)
         z = lax.axis_index("z")
         spot = 2 * z + core
@@ -1112,8 +1132,8 @@
         mine = lax.dynamic_index_in_dim(mine, 2 * y + x, 1, keepdims=False)
         grad_upb = lax.dynamic_slice_in_dim(mine, spot * f_up, f_up, 2)
         ended = {
-            kind: [streams[kind, layer]["held"].astype(jnp.float32) for layer in range(LAYERS)]
-            for kind in ("att", "mlp")
+            kind: [streams[kind, layer].held.astype(jnp.float32) for layer in range(LAYERS)]
+            for kind in (ATT, MLP)
         }
 
         def unpack(grad):
@@ -1123,12 +1143,12 @@
         return (
             full_out,
             full_back,
-            jnp.stack([unpack(grad) for grad in ended["att"]]),
+            jnp.stack([unpack(grad) for grad in ended[ATT]]),
             grad_qv,
-            jnp.stack([grad[:, 3 * local :].T for grad in ended["att"]]),
-            jnp.stack([grad[:, :units] for grad in ended["mlp"]]),
+            jnp.stack([grad[:, 3 * local :].T for grad in ended[ATT]]),
+            jnp.stack([grad[:, :units] for grad in ended[MLP]]),
             grad_upb,
-            jnp.stack([grad[:, units:].T for grad in ended["mlp"]]),
+            jnp.stack([grad[:, units:].T for grad in ended[MLP]]),
             grad_gain,
             grad_shift,
         )

time: 867 us -> 848 us (0.978)
  waiting for transfers between devices: 299 us -> 280 us
    ppermute x5 -> x2, waiting for transfers between devices: 39.7 us -> 7.49 us  [total_of(): table = table + lax.ppermute(table, CELLS[0], partner)]
    ppermute x28 -> x30, waiting for transfers between devices: 111 us -> 123 us  [move(): return lax.ppermute(values, CELLS, moves)]
    unnamed x328 -> x298, local copies, waits for them, and re-layouts: 28 us -> 32 us
    ppermute x28 -> x30, starting transfers between devices: 41 us -> 42.7 us  [move(): return lax.ppermute(values, CELLS, moves)]
    ppermute x26 -> x28, starting transfers between devices: 33.4 us -> 31.7 us  [flip(): return lax.ppermute(values, 'core', FLIP)]
  transfers between devices with their start and end apart: 81 -> 82, of which waited for: 28 -> 29; matrix products, arithmetic and copies ran while one was open for 34% -> 34% of each run, Pallas kernels for 10% -> 10%
where the time goes in v2:
time: 848 us; the launch traced here: 838 us
  waiting for transfers between devices  280 us (33%)
  matrix products  147 us (17%)
  other arithmetic  105 us (12%)
  starting transfers between devices  94.1 us (11%)
  Pallas kernels  86.9 us (10%)
  local copies, waits for them, and re-layouts  82.4 us (10%)
  blocking collectives  25.2 us (3%)
  between operations  17.1 us (2%)
    dot_general x56, matrix products, product(): lax.dot_general(left, right, dims, preferred_element_type=jnp.float32)  147 us
    ppermute x30, waiting for transfers between devices, move(): return lax.ppermute(values, CELLS, moves)  123 us
    pallas_call x8, Pallas kernels, kernel_call(): pl.pallas_call(kernel, grid=(pairs,), in_specs=[pl.BlockSpec(memory_space...  73.7 us
    ppermute x4, waiting for transfers between devices, gather_quad(): across = lax.ppermute(values, 'x', FLIP)  71.1 us
    ppermute x4, waiting for transfers between devices, reduce_quad(): across = lax.ppermute(across, 'x', FLIP)  57.4 us
    ppermute x30, starting transfers between devices, move(): return lax.ppermute(values, CELLS, moves)  42.7 us
    unnamed x298, local copies, waits for them, and re-layouts  32 us
    ppermute x28, starting transfers between devices, flip(): return lax.ppermute(values, 'core', FLIP)  31.7 us
  transfers between devices with their start and end apart: 82, of which 29 were waited for; matrix products, arithmetic and copies ran while one was open for 34% of the time, Pallas kernels for 10%

profile of v2, /device:TPU:0, one launch (start us, length us, event | category | flops | bytes accessed | tf_op | source)
XLA Modules:
  0.0 838.0 jit_solution(21762714257803710)
XLA Ops:
  12.7 15.7 %all-gather = f32[192,32]{1,0:T(8,128)S(1)} all-gather(f32[24,32]{1,0:T(8,128)S(1)} %pad_maximum_fusion.26), channel_id=2, replica_groups=mesh['z'=4,'core'=2,'y'=2,'x'=2] {'z','core'}, dimensions={0}, use_global_device_ids=true | all-gather | bytes 27648 | tf_op jit(solution)/shard_map/all_gather | solution.py:896
  28.4 9.5 %all-gather.1 = f32[32,24,32]{2,1,0:T(8,128)S(1)} all-gather(f32[8,24,32]{2,1,0:T(8,128)S(1)} %bitcast.251), channel_id=3, replica_groups=mesh['z'=4,'core'=2,'y'=2,'x'=2] {'y','x'}, dimensions={0}, use_global_device_ids=true | all-gather | bytes 122880 | tf_op jit(solution)/shard_map/all_gather | solution.py:897
  66.5 18.8 %collective-permute-done.2 = bf16[1024,1024]{1,0:T(8,128)(2,1)} collective-permute-done((bf16[1024,1024]{1,0:T(8,128)(2,1)}, bf16[1024,1024]{1,0:T(8,128)(2,1)}, u32[]{:S(2)}, u32[]{:S(2)}) %collective-permute-start.2) | collective-permute-done | bytes 2097184 | tf_op jit(solution)/shard_map/ppermute | solution.py:708
  115.6 8.1 shard_map.177
  127.4 6.4 shard_map.178
  160.6 20.3 %collective-permute-done.8 = bf16[448,1024]{1,0:T(8,128)(2,1)} collective-permute-done((bf16[448,1024]{1,0:T(8,128)(2,1)S(1)}, bf16[448,1024]{1,0:T(8,128)(2,1)}, u32[]{:S(2)}, u32[]{:S(2)}) %collective-permute-start.8) | collective-permute-done | bytes 917536 | tf_op jit(solution)/shard_map/ppermute | solution.py:764
  192.3 6.3 multiply_convert_fusion.1
  198.7 30.9 %collective-permute-done.12 = bf16[1024,1024]{1,0:T(8,128)(2,1)} collective-permute-done((bf16[1024,1024]{1,0:T(8,128)(2,1)}, bf16[1024,1024]{1,0:T(8,128)(2,1)}, u32[]{:S(2)}, u32[]{:S(2)}) %collective-permute-start.12) | collective-permute-done | bytes 2097184 | tf_op jit(solution)/shard_map/ppermute | solution.py:708
  244.7 13.3 %collective-permute-done.15 = bf16[448,1024]{1,0:T(8,128)(2,1)S(1)} collective-permute-done((bf16[448,1024]{1,0:T(8,128)(2,1)S(1)}, bf16[448,1024]{1,0:T(8,128)(2,1)S(1)}, u32[]{:S(2)}, u32[]{:S(2)}) %collective-permute-start.15) | collective-permute-done | bytes 917536 | tf_op jit(solution)/shard_map/ppermute | solution.py:774
  281.1 8.1 shard_map.179
  292.0 6.4 shard_map.180
  324.8 14.5 %collective-permute-done.26 = bf16[448,1024]{1,0:T(8,128)(2,1)} collective-permute-done((bf16[448,1024]{1,0:T(8,128)(2,1)S(1)}, bf16[448,1024]{1,0:T(8,128)(2,1)}, u32[]{:S(2)}, u32[]{:S(2)}) %collective-permute-start.26) | collective-permute-done | bytes 917536 | tf_op jit(solution)/shard_map/ppermute | solution.py:764
  343.5 14.4 %collective-permute-done.23 = bf16[448,1024]{1,0:T(8,128)(2,1)} collective-permute-done((bf16[448,1024]{1,0:T(8,128)(2,1)}, bf16[448,1024]{1,0:T(8,128)(2,1)}, u32[]{:S(2)}, u32[]{:S(2)}) %collective-permute-start.23) | collective-permute-done | bytes 917536 | tf_op jit(solution)/shard_map/ppermute | solution.py:764
  362.3 6.9 multiply_convert_fusion
  369.5 13.6 %fusion.10 = (f32[1024]{0:T(1024)}, bf16[1792,1024]{1,0:T(8,128)(2,1)S(1)}, f32[1792,1024]{1,0:T(8,128)S(1)}) fusion(f32[1792,1024]{1,0:T(8,128)} %get-tuple-element.359, f32[1024]{0:T(1024)S(1)} %add.574, bf16[1024,1024]{1,0:T(8,128)(2,1)S(1)} %broadcast_select_fusion, bf16[448,1024]{1,0:T(8,128)(2,1)S(1)} %collective-permute-done.24, ...), kind=kOutput, calls=%fused_computation.17 | convolution fusion | flops 3796630528 | bytes 24125440 | tf_op jit(solution)/shard_map/dot_general | solution.py:413
  395.3 6.9 convolution_convert_fusion.2
  403.5 13.0 %collective-permute-done.32 = bf16[448,1024]{1,0:T(8,128)(2,1)S(1)} collective-permute-done((bf16[448,1024]{1,0:T(8,128)(2,1)S(1)}, bf16[448,1024]{1,0:T(8,128)(2,1)S(1)}, u32[]{:S(2)}, u32[]{:S(2)}) %collective-permute-start.32) | collective-permute-done | bytes 917536 | tf_op jit(solution)/shard_map/ppermute | solution.py:774
  434.3 18.6 %collective-permute-done.35 = bf16[448,1024]{1,0:T(8,128)(2,1)S(1)} collective-permute-done((bf16[448,1024]{1,0:T(8,128)(2,1)S(1)}, bf16[448,1024]{1,0:T(8,128)(2,1)S(1)}, u32[]{:S(2)}, u32[]{:S(2)}) %collective-permute-start.35) | collective-permute-done | bytes 917536 | tf_op jit(solution)/shard_map/ppermute | solution.py:774
  463.0 9.3 %shard_map.182 = (f32[304,768]{1,0:T(8,128)}, f32[304,768]{1,0:T(8,128)}, bf16[304,512]{1,0:T(8,128)(2,1)}, bf16[304,512]{1,0:T(8,128)(2,1)}, f32[2,8,128]{2,1,0:T(8,128)}) custom-call(s32[4]{0:T(128)} %pad_add_fusion.place, bf16[896,768]{1,0:T(8,128)(2,1)} %copy-done.9, bf16[896,768]{1,0:T(8,128)(2,1)} %copy-done.10, ...), custom_call_target="tpu_custom_call" | custom-call | tf_op jit(solution)/shard_map/pallas_call | solution.py:560
  475.0 13.2 %shard_map.183 = (bf16[896,768]{1,0:T(8,128)(2,1)}, bf16[896,768]{1,0:T(8,128)(2,1)}, f32[2,8,128]{2,1,0:T(8,128)}) custom-call(s32[4]{0:T(128)} %pad_add_fusion.place, bf16[896,768]{1,0:T(8,128)(2,1)} %copy-done.9, bf16[896,768]{1,0:T(8,128)(2,1)} %copy-done.10, bf16[896,256]{1,0:T(8,128)(2,1)} %convolution_convert_fusion.23.up_a, ...), custom_call_target="tpu_custom_call" | custom-call | tf_op jit(solution)/shard_map/pallas_call | solution.py:560
  509.8 21.9 %collective-permute-done.46 = bf16[448,1024]{1,0:T(8,128)(2,1)} collective-permute-done((bf16[448,1024]{1,0:T(8,128)(2,1)S(1)}, bf16[448,1024]{1,0:T(8,128)(2,1)}, u32[]{:S(2)}, u32[]{:S(2)}) %collective-permute-start.46) | collective-permute-done | bytes 917536 | tf_op jit(solution)/shard_map/ppermute | solution.py:764
  531.7 7.1 fusion.9
  568.8 12.6 %collective-permute-done.50 = bf16[448,1024]{1,0:T(8,128)(2,1)S(1)} collective-permute-done((bf16[448,1024]{1,0:T(8,128)(2,1)S(1)}, bf16[448,1024]{1,0:T(8,128)(2,1)S(1)}, u32[]{:S(2)}, u32[]{:S(2)}) %collective-permute-start.50) | collective-permute-done | bytes 917536 | tf_op jit(solution)/shard_map/ppermute | solution.py:774
  584.1 9.5 %collective-permute-start.53 = (bf16[448,1024]{1,0:T(8,128)(2,1)S(1)}, bf16[448,1024]{1,0:T(8,128)(2,1)S(1)}, u32[]{:S(2)}, u32[]{:S(2)}) collective-permute-start(bf16[448,1024]{1,0:T(8,128)(2,1)S(1)} %convert_element_type.381), channel_id=1, source_target_pairs={{0,4},{4,0},{1,5},{5,1},{2,6},{6,2},{3,7},{7,3},{8,12},{12,8},{9,1... | collective-permute-start | bytes 2752520 | tf_op jit(solution)/shard_map/ppermute | solution.py:796
  607.8 9.3 %shard_map.184 = (f32[304,768]{1,0:T(8,128)}, f32[304,768]{1,0:T(8,128)}, bf16[304,512]{1,0:T(8,128)(2,1)}, bf16[304,512]{1,0:T(8,128)(2,1)}, f32[2,8,128]{2,1,0:T(8,128)}) custom-call(s32[4]{0:T(128)} %pad_add_fusion.place, bf16[896,768]{1,0:T(8,128)(2,1)} %copy-done.7, bf16[896,768]{1,0:T(8,128)(2,1)} %copy-done.8, ...), custom_call_target="tpu_custom_call" | custom-call | tf_op jit(solution)/shard_map/pallas_call | solution.py:560
  619.7 8.3 convolution_convert_fusion
  628.0 13.0 %shard_map.185 = (bf16[896,768]{1,0:T(8,128)(2,1)}, bf16[896,768]{1,0:T(8,128)(2,1)}, f32[2,8,128]{2,1,0:T(8,128)}) custom-call(s32[4]{0:T(128)} %pad_add_fusion.place, bf16[896,768]{1,0:T(8,128)(2,1)} %copy-done.7, bf16[896,768]{1,0:T(8,128)(2,1)} %copy-done.8, bf16[896,256]{1,0:T(8,128)(2,1)} %convolution_convert_fusion.21.up_a, ...), custom_call_target="tpu_custom_call" | custom-call | tf_op jit(solution)/shard_map/pallas_call | solution.py:560
  735.8 15.3 %collective-permute-done.39.round_11 = bf16[448,1024]{1,0:T(8,128)(2,1)S(1)} collective-permute-done((bf16[448,1024]{1,0:T(8,128)(2,1)S(1)}, bf16[448,1024]{1,0:T(8,128)(2,1)S(1)}, u32[]{:S(2)}, u32[]{:S(2)}) %collective-permute-start.39) | collective-permute-done | bytes 917536 | tf_op jit(solution)/shard_map/ppermute | solution.py:708
  753.2 18.2 %collective-permute-done.38.round_10 = bf16[448,1024]{1,0:T(8,128)(2,1)S(1)} collective-permute-done((bf16[448,1024]{1,0:T(8,128)(2,1)S(1)}, bf16[448,1024]{1,0:T(8,128)(2,1)S(1)}, u32[]{:S(2)}, u32[]{:S(2)}) %collective-permute-start.38) | collective-permute-done | bytes 917536 | tf_op jit(solution)/shard_map/ppermute | solution.py:708
  777.2 6.7 shard_map.181
  791.2 20.2 %collective-permute-done.62.round_01 = bf16[448,1024]{1,0:T(8,128)(2,1)} collective-permute-done((bf16[448,1024]{1,0:T(8,128)(2,1)S(1)}, bf16[448,1024]{1,0:T(8,128)(2,1)}, u32[]{:S(2)}, u32[]{:S(2)}) %collective-permute-start.62) | collective-permute-done | bytes 917536 | tf_op jit(solution)/shard_map/ppermute | solution.py:708
  811.4 6.5 shard_map.186
  (732 shorter events, 418.1 us)
Async XLA Ops:
  7.2 36.5 %all-gather.9.cloned.1.call-start = ((), (), s32[]{:S(2)}) async-start(), calls=%async_computation.4 | async-start | bytes 2359296 | tf_op jit(solution)/shard_map/all_gather | solution.py:877
  11.5 148.0 %all-gather.11.cloned.1.call-start = ((), (), s32[]{:S(2)}) async-start(), calls=%async_computation.5 | async-start | bytes 2359296 | tf_op jit(solution)/shard_map/all_gather | solution.py:877
  12.4 170.1 %all-gather.13.cloned.1.call-start = ((), (), s32[]{:S(2)}) async-start(), calls=%async_computation.6 | async-start | bytes 2359296 | tf_op jit(solution)/shard_map/all_gather | solution.py:877
  56.4 127.1 %all-gather.15.cloned.1.call-start = ((), (), s32[]{:S(2)}) async-start(), calls=%async_computation.7 | async-start | bytes 2359296 | tf_op jit(solution)/shard_map/all_gather | solution.py:877
  65.4 28.1 %collective-permute-start.1 = (bf16[448,1024]{1,0:T(8,128)(2,1)S(1)}, bf16[448,1024]{1,0:T(8,128)(2,1)}, u32[]{:S(2)}, u32[]{:S(2)}) collective-permute-start(bf16[448,1024]{1,0:T(8,128)(2,1)S(1)} %add_convert_fusion.15), channel_id=1, source_target_pairs={{0,4},{4,0},{1,5},{5,1},{2,6},{6,2},{3,7},{7,3},{8,12},{12,8},{9,1... | collective-permute-start | bytes 2752520 | tf_op jit(solution)/shard_map/ppermute | solution.py:796
  142.4 175.0 %all-gather.19.cloned.1.call-start = ((), (), s32[]{:S(2)}) async-start(), calls=%async_computation.9 | async-start | bytes 2359296 | tf_op jit(solution)/shard_map/all_gather | solution.py:877
  159.4 31.1 %collective-permute-start.11 = (bf16[1024,1024]{1,0:T(8,128)(2,1)}, bf16[1024,1024]{1,0:T(8,128)(2,1)}, u32[]{:S(2)}, u32[]{:S(2)}) collective-permute-start(bf16[1024,1024]{1,0:T(8,128)(2,1)} %all-gather.11.cloned.1.call-done), channel_id=1, source_target_pairs={{0,2},{1,3},{2,6},{3,7},{4,0},{5,1},{6,4},{7,5},{8,10},{9,11},{10,... | collective-permute-start | bytes 6291464 | tf_op jit(solution)/shard_map/ppermute | solution.py:708
  160.6 27.8 %collective-permute-start.7 = (bf16[448,1024]{1,0:T(8,128)(2,1)S(1)}, bf16[448,1024]{1,0:T(8,128)(2,1)}, u32[]{:S(2)}, u32[]{:S(2)}) collective-permute-start(bf16[448,1024]{1,0:T(8,128)(2,1)S(1)} %copy-done.34), channel_id=1, source_target_pairs={{0,4},{4,0},{1,5},{5,1},{2,6},{6,2},{3,7},{7,3},{8,12},{12,8},{9,1... | collective-permute-start | bytes 2752520 | tf_op jit(solution)/shard_map/ppermute | solution.py:796
  182.5 47.1 %collective-permute-start.12 = (bf16[1024,1024]{1,0:T(8,128)(2,1)}, bf16[1024,1024]{1,0:T(8,128)(2,1)}, u32[]{:S(2)}, u32[]{:S(2)}) collective-permute-start(bf16[1024,1024]{1,0:T(8,128)(2,1)} %all-gather.13.cloned.1.call-done), channel_id=1, source_target_pairs={{0,2},{1,3},{2,6},{3,7},{4,0},{5,1},{6,4},{7,5},{8,10},{9,11},{10,... | collective-permute-start | bytes 6291464 | tf_op jit(solution)/shard_map/ppermute | solution.py:708
  183.5 52.7 %collective-permute-start.17 = (bf16[1024,1024]{1,0:T(8,128)(2,1)}, bf16[1024,1024]{1,0:T(8,128)(2,1)S(1)}, u32[]{:S(2)}, u32[]{:S(2)}) collective-permute-start(bf16[1024,1024]{1,0:T(8,128)(2,1)} %all-gather.15.cloned.1.call-done), channel_id=1, source_target_pairs={{0,1},{1,0},{2,3},{3,2},{4,6},{5,7},{6,4},{7,5},{8,9},{9,8},{10,11... | collective-permute-start | bytes 6291464 | tf_op jit(solution)/shard_map/ppermute | solution.py:708
  260.2 81.6 %all-gather.17.cloned.1.call-start = ((), (), s32[]{:S(2)}) async-start(), calls=%async_computation.8 | async-start | bytes 2359296 | tf_op jit(solution)/shard_map/all_gather | solution.py:877
  310.7 339.1 %reduce-scatter.5.cloned.1.call-start = ((), (), s32[]{:S(2)}) async-start(), calls=%async_computation.10 | async-start | bytes 4718592 | tf_op jit(solution)/shard_map/reduce_scatter | solution.py:743
  317.4 43.0 %collective-permute-start.28 = (bf16[1024,1024]{1,0:T(8,128)(2,1)}, bf16[1024,1024]{1,0:T(8,128)(2,1)}, u32[]{:S(2)}, u32[]{:S(2)}) collective-permute-start(bf16[1024,1024]{1,0:T(8,128)(2,1)} %all-gather.19.cloned.1.call-done), channel_id=1, source_target_pairs={{0,2},{1,3},{2,6},{3,7},{4,0},{5,1},{6,4},{7,5},{8,10},{9,11},{10,... | collective-permute-start | bytes 6291464 | tf_op jit(solution)/shard_map/ppermute | solution.py:708
  324.1 33.8 %collective-permute-start.23 = (bf16[448,1024]{1,0:T(8,128)(2,1)}, bf16[448,1024]{1,0:T(8,128)(2,1)}, u32[]{:S(2)}, u32[]{:S(2)}) collective-permute-start(bf16[448,1024]{1,0:T(8,128)(2,1)} %convert_element_type.335), channel_id=1, source_target_pairs={{0,1},{1,0},{2,3},{3,2},{4,5},{5,4},{6,7},{7,6},{8,9},{9,8},{10,11... | collective-permute-start | bytes 2752520 | tf_op jit(solution)/shard_map/ppermute | solution.py:764
  324.8 33.2 %collective-permute-start.25 = (bf16[448,1024]{1,0:T(8,128)(2,1)S(1)}, bf16[448,1024]{1,0:T(8,128)(2,1)}, u32[]{:S(2)}, u32[]{:S(2)}) collective-permute-start(bf16[448,1024]{1,0:T(8,128)(2,1)S(1)} %add_convert_fusion.10), channel_id=1, source_target_pairs={{0,4},{4,0},{1,5},{5,1},{2,6},{6,2},{3,7},{7,3},{8,12},{12,8},{9,1... | collective-permute-start | bytes 2752520 | tf_op jit(solution)/shard_map/ppermute | solution.py:796
  402.2 86.0 %collective-permute-start.42 = (bf16[1024,1024]{1,0:T(8,128)(2,1)}, bf16[1024,1024]{1,0:T(8,128)(2,1)}, u32[]{:S(2)}, u32[]{:S(2)}) collective-permute-start(bf16[1024,1024]{1,0:T(8,128)(2,1)} %convolution_convert_fusion.2), channel_id=1, source_target_pairs={{0,4},{1,5},{2,0},{3,1},{4,6},{5,7},{6,2},{7,3},{8,12},{9,13},{10,... | collective-permute-start | bytes 6291464 | tf_op jit(solution)/shard_map/ppermute | solution.py:708
  424.4 63.8 %collective-permute-start.41 = (bf16[1024,1024]{1,0:T(8,128)(2,1)}, bf16[1024,1024]{1,0:T(8,128)(2,1)S(1)}, u32[]{:S(2)}, u32[]{:S(2)}) collective-permute-start(bf16[1024,1024]{1,0:T(8,128)(2,1)} %convolution_convert_fusion.3), channel_id=1, source_target_pairs={{0,4},{1,5},{2,0},{3,1},{4,6},{5,7},{6,2},{7,3},{8,12},{9,13},{10,... | collective-permute-start | bytes 6291464 | tf_op jit(solution)/shard_map/ppermute | solution.py:708
  509.7 33.4 %collective-permute-start.45 = (bf16[448,1024]{1,0:T(8,128)(2,1)S(1)}, bf16[448,1024]{1,0:T(8,128)(2,1)}, u32[]{:S(2)}, u32[]{:S(2)}) collective-permute-start(bf16[448,1024]{1,0:T(8,128)(2,1)S(1)} %convert_element_type.369), channel_id=1, source_target_pairs={{0,4},{4,0},{1,5},{5,1},{2,6},{6,2},{3,7},{7,3},{8,12},{12,8},{9,1... | collective-permute-start | bytes 2752520 | tf_op jit(solution)/shard_map/ppermute | solution.py:796
  538.9 279.0 %reduce-scatter.9.cloned.1.call-start = ((), (), s32[]{:S(2)}) async-start(), calls=%async_computation.12 | async-start | bytes 2359296 | tf_op jit(solution)/shard_map/reduce_scatter | solution.py:743
  599.0 81.3 %collective-permute-start.57 = (bf16[1024,1024]{1,0:T(8,128)(2,1)}, bf16[1024,1024]{1,0:T(8,128)(2,1)}, u32[]{:S(2)}, u32[]{:S(2)}) collective-permute-start(bf16[1024,1024]{1,0:T(8,128)(2,1)} %convolution_convert_fusion.1), channel_id=1, source_target_pairs={{0,4},{1,5},{2,0},{3,1},{4,6},{5,7},{6,2},{7,3},{8,12},{9,13},{10,... | collective-permute-start | bytes 6291464 | tf_op jit(solution)/shard_map/ppermute | solution.py:708
  602.3 43.8 %collective-permute-start.54 = (bf16[1024,1024]{1,0:T(8,128)(2,1)}, bf16[1024,1024]{1,0:T(8,128)(2,1)}, u32[]{:S(2)}, u32[]{:S(2)}) collective-permute-start(bf16[1024,1024]{1,0:T(8,128)(2,1)} %fusion.32), channel_id=1, source_target_pairs={{0,1},{1,0},{2,3},{3,2},{4,6},{5,7},{6,4},{7,5},{8,9},{9,8},{10,11... | collective-permute-start | bytes 6291464 | tf_op jit(solution)/shard_map/ppermute | solution.py:708
  628.0 52.3 %collective-permute-start.58 = (bf16[1024,1024]{1,0:T(8,128)(2,1)}, bf16[1024,1024]{1,0:T(8,128)(2,1)}, u32[]{:S(2)}, u32[]{:S(2)}) collective-permute-start(bf16[1024,1024]{1,0:T(8,128)(2,1)} %convolution_convert_fusion), channel_id=1, source_target_pairs={{0,4},{1,5},{2,0},{3,1},{4,6},{5,7},{6,2},{7,3},{8,12},{9,13},{10,... | collective-permute-start | bytes 6291464 | tf_op jit(solution)/shard_map/ppermute | solution.py:708
  649.8 173.2 %reduce-scatter.7.cloned.1.call-start = ((), (), s32[]{:S(2)}) async-start(), calls=%async_computation.11 | async-start | bytes 2359296 | tf_op jit(solution)/shard_map/reduce_scatter | solution.py:743
  695.5 28.5 %collective-permute-start.71 = (bf16[1024,1024]{1,0:T(8,128)(2,1)}, bf16[1024,1024]{1,0:T(8,128)(2,1)}, u32[]{:S(2)}, u32[]{:S(2)}) collective-permute-start(bf16[1024,1024]{1,0:T(8,128)(2,1)} %fusion.33), channel_id=1, source_target_pairs={{0,1},{1,0},{2,3},{3,2},{4,6},{5,7},{6,4},{7,5},{8,9},{9,8},{10,11... | collective-permute-start | bytes 6291464 | tf_op jit(solution)/shard_map/ppermute | solution.py:708
  727.6 99.6 %reduce-scatter.11.cloned.1.call-start = ((), (), s32[]{:S(2)}) async-start(), calls=%async_computation.13 | async-start | bytes 4718592 | tf_op jit(solution)/shard_map/reduce_scatter | solution.py:743
  729.5 41.9 %collective-permute-start.38 = (bf16[448,1024]{1,0:T(8,128)(2,1)S(1)}, bf16[448,1024]{1,0:T(8,128)(2,1)S(1)}, u32[]{:S(2)}, u32[]{:S(2)}) collective-permute-start(bf16[448,1024]{1,0:T(8,128)(2,1)S(1)} %copy-done.29), channel_id=1, source_target_pairs={{0,1},{1,0},{2,5},{3,4},{4,3},{5,2},{6,7},{7,6},{8,9},{9,8},{10,13... | collective-permute-start | bytes 2752520 | tf_op jit(solution)/shard_map/ppermute | solution.py:708
  730.5 41.8 %collective-permute-start.36 = (bf16[448,1024]{1,0:T(8,128)(2,1)S(1)}, bf16[448,1024]{1,0:T(8,128)(2,1)S(1)}, u32[]{:S(2)}, u32[]{:S(2)}) collective-permute-start(bf16[448,1024]{1,0:T(8,128)(2,1)S(1)} %copy-done.29), channel_id=1, source_target_pairs={{2,4},{3,5},{4,2},{5,3},{10,12},{11,13},{12,10},{13,11},{18,20},{1... | collective-permute-start | bytes 2752520 | tf_op jit(solution)/shard_map/ppermute | solution.py:708
  731.3 45.9 %collective-permute-start.37 = (bf16[448,1024]{1,0:T(8,128)(2,1)S(1)}, bf16[448,1024]{1,0:T(8,128)(2,1)}, u32[]{:S(2)}, u32[]{:S(2)}) collective-permute-start(bf16[448,1024]{1,0:T(8,128)(2,1)S(1)} %copy-done.29), channel_id=1, source_target_pairs={{0,2},{1,3},{2,6},{3,7},{4,0},{5,1},{6,4},{7,5},{8,10},{9,11},{10,... | collective-permute-start | bytes 2752520 | tf_op jit(solution)/shard_map/ppermute | solution.py:708
  734.2 49.8 %collective-permute-start.61 = (bf16[448,1024]{1,0:T(8,128)(2,1)S(1)}, bf16[448,1024]{1,0:T(8,128)(2,1)}, u32[]{:S(2)}, u32[]{:S(2)}) collective-permute-start(bf16[448,1024]{1,0:T(8,128)(2,1)S(1)} %copy-done.35), channel_id=1, source_target_pairs={{2,4},{3,5},{4,2},{5,3},{10,12},{11,13},{12,10},{13,11},{18,20},{1... | collective-permute-start | bytes 2752520 | tf_op jit(solution)/shard_map/ppermute | solution.py:708
  751.2 40.0 %collective-permute-start.63 = (bf16[448,1024]{1,0:T(8,128)(2,1)S(1)}, bf16[448,1024]{1,0:T(8,128)(2,1)}, u32[]{:S(2)}, u32[]{:S(2)}) collective-permute-start(bf16[448,1024]{1,0:T(8,128)(2,1)S(1)} %copy-done.35), channel_id=1, source_target_pairs={{0,1},{1,0},{2,5},{3,4},{4,3},{5,2},{6,7},{7,6},{8,9},{9,8},{10,13... | collective-permute-start | bytes 2752520 | tf_op jit(solution)/shard_map/ppermute | solution.py:708
  771.4 40.0 %collective-permute-start.62 = (bf16[448,1024]{1,0:T(8,128)(2,1)S(1)}, bf16[448,1024]{1,0:T(8,128)(2,1)}, u32[]{:S(2)}, u32[]{:S(2)}) collective-permute-start(bf16[448,1024]{1,0:T(8,128)(2,1)S(1)} %copy-done.35), channel_id=1, source_target_pairs={{0,2},{1,3},{2,6},{3,7},{4,0},{5,1},{6,4},{7,5},{8,10},{9,11},{10,... | collective-permute-start | bytes 2752520 | tf_op jit(solution)/shard_map/ppermute | solution.py:708
  772.3 39.1 %collective-permute-start.64 = (bf16[448,1024]{1,0:T(8,128)(2,1)S(1)}, bf16[448,1024]{1,0:T(8,128)(2,1)}, u32[]{:S(2)}, u32[]{:S(2)}) collective-permute-start(bf16[448,1024]{1,0:T(8,128)(2,1)S(1)} %copy-done.35), channel_id=1, source_target_pairs={{0,3},{1,2},{2,7},{3,6},{4,1},{5,0},{6,5},{7,4},{8,11},{9,10},{10,... | collective-permute-start | bytes 2752520 | tf_op jit(solution)/shard_map/ppermute | solution.py:708
  (183 other events, 1765.1 us)
Sparse Core Ops, SparseCore 0:
  11.6 32.1 all-gather.8
  45.3 28.4 all-gather.10
  75.5 28.5 all-gather.12
  142.5 27.8 all-gather.14
  260.4 31.0 all-gather.18
  310.8 31.0 all-gather.16
  539.0 47.9 reduce-scatter.4
  649.9 38.2 reduce-scatter.8
  727.7 34.7 reduce-scatter.6
  764.7 48.4 reduce-scatter.10
